TPU v7x, 256 devices: a whole 4x4x8 slice. The times are simulated.
256 devices in a mesh: img: 32 (over y, z), ori: 8 (over x, core).
Axes of the slice: x: 4, y: 4, z: 8, core: 2. Of those that a mesh axis runs over, the one named last changes fastest.
Arguments:
- images: bfloat16 [1024, 2, 16256], P('img'), may hold values from -6 to 6
- shifts: int32 [1024], P('img'), may hold values from 0 to 35
- inv_temp: float32 [1024], P('img'), may hold values from 0.5 to 4
- candidates: int32 [32, 512], P('img'), may hold values from 0 to 1023
- volume: bfloat16 [64, 2, 16256], P(None, None, 'img'), may hold values from -6 to 6
- tilts: bfloat16 [1024, 64], P('ori'), may hold values from -1 to 1
- azimuth: float32 [1024], P('ori'), may hold values from -3.140625 to 3.140625
Outputs:
- posteriors: float32 [1024, 1024], P('img', 'ori')
- weighted_sums: float32 [16256, 2, 1024], P('img', None, 'ori')
- volume_grad: float32 [64, 2, 16256], P(None, None, 'img')
Inputs may be any that keep to these rules, and one draw needn't show every extreme that they name: `candidates`: A group's list may name an orientation more than once.
All inputs are finite; a program needn't handle non-finite values.
Results may differ from a plain program's by a relative error of at most 0.017.
Values may be sent and summed in bfloat16 or wider, within the bound.
No kernel may reach another device: no remote copies, remote signals or barrier semaphores. Data moves between devices by JAX's collectives and lax.ppermute only.
A program may use at most 128 MiB of HBM per device.

v0:
```python
import math

import jax
import jax.numpy as jnp
from jax import lax
from jax.experimental import pallas as pl
from jax.experimental.pallas import tpu as pltpu
from jax.sharding import Mesh
from jax.sharding import PartitionSpec as P


NSHIFT = 36
LANES = 128
ROWS = 8
ORDERS = 64
noise_var = 128.0
masked_fill = -1e30
ORI = ("x", "c")


def call(kernel, out_shape, scalars, *args, flops=0):
    specs = [pl.BlockSpec(memory_space=pltpu.SMEM)] + [pl.BlockSpec(memory_space=pltpu.VMEM)] * len(args)
    outs = jax.tree.map(lambda _: pl.BlockSpec(memory_space=pltpu.VMEM), out_shape)
    moved = sum(a.size * a.dtype.itemsize for a in (*args, *jax.tree.leaves(out_shape)))
    return pl.pallas_call(
        kernel,
        out_shape=out_shape,
        in_specs=specs,
        out_specs=outs,
        compiler_params=pltpu.CompilerParams(vmem_limit_bytes=8 * 2**20),
        cost_estimate=pl.CostEstimate(flops=flops, transcendentals=0, bytes_accessed=moved),
    )(scalars, *args)


def shape(dims, dtype=jnp.float32):
    return jax.ShapeDtypeStruct(dims, dtype)


def across(x, axis, step):
    count = lax.axis_size(axis)
    return lax.ppermute(x, axis, [(s, (s + step) % count) for s in range(count)])


def orders(start):
    lane = lax.broadcasted_iota(jnp.int32, (1, LANES), 1)
    return ((start + lane) % ORDERS - ORDERS // 2).astype(jnp.float32)


def rotate_and_cut(width, parts):
    tiles = -(-width // LANES)

    def kernel(s_ref, shifts_ref, images_ref, out_ref):
        c, x = s_ref[0], s_ref[1]
        row = lax.broadcasted_iota(jnp.int32, (ROWS, LANES), 0)
        phase = jnp.zeros((ROWS, LANES), jnp.float32)
        for n in range(ROWS):
            phase = jnp.where(row == n, shifts_ref[x * ROWS + n].astype(jnp.float32), phase)
        angles = phase * (2.0 * math.pi / NSHIFT) * orders(0)
        cosine, sine = jnp.cos(angles), jnp.sin(angles)
        a = jnp.where(c == 0, cosine, sine)
        b = jnp.where(c == 0, -sine, cosine)
        lane = lax.broadcasted_iota(jnp.int32, (ROWS, LANES), 1)
        whole = images_ref.shape[2] // LANES
        turned = []
        for k in range(whole):
            at = slice(k * LANES, (k + 1) * LANES)
            both = images_ref[:, :, at].astype(jnp.float32)
            turned.append(both[:, 0, :] * a + both[:, 1, :] * b)
        for part in range(parts):
            shift = (part * width) % LANES
            for t in range(tiles):
                first = part * width // LANES + t
                one = turned[first]
                if shift:
                    two = turned[min(first + 1, whole - 1)]
                    one = jnp.where(lane < shift, two, one)
                    one = pltpu.roll(one, LANES - shift, 1)
                left = width - t * LANES
                if left < LANES:
                    one = jnp.where(lane < left, one, 0.0)
                out_ref[part, t] = one.astype(jnp.bfloat16)

    return kernel


def cut_images(images, shifts, scalars, width, parts):
    tiles = -(-width // LANES)
    return pl.pallas_call(
        rotate_and_cut(width, parts),
        out_shape=shape((parts, tiles, ROWS, LANES), jnp.bfloat16),
        grid_spec=pltpu.PrefetchScalarGridSpec(
            num_scalar_prefetch=2,
            grid=(1,),
            in_specs=[pl.BlockSpec((ROWS, 2, images.shape[2]), lambda g, s, n: (s[1], 0, 0))],
            out_specs=pl.BlockSpec((parts, tiles, ROWS, LANES), lambda g, s, n: (0, 0, 0, 0)),
        ),
        compiler_params=pltpu.CompilerParams(vmem_limit_bytes=60 * 2**20),
    )(scalars, shifts, images)


def slices_kernel(width):
    def kernel(s_ref, packed_ref, volume_ref, slices_ref, half_ref, cos_ref, sin_ref):
        degrees = volume_ref.shape[1]
        order = orders(s_ref[2] * width)
        for d in range(packed_ref.shape[0]):
            block = packed_ref[d].T
            angles = jnp.broadcast_to(block[:, degrees : degrees + 1], block.shape) * order
            cosine, sine = jnp.cos(angles), jnp.sin(angles)
            if d == 0:
                cos_ref[...] = cosine
                sin_ref[...] = sine
            tilts = block[:, :degrees].astype(jnp.bfloat16)
            power = jnp.zeros_like(block)
            for t in range(volume_ref.shape[2] // LANES):
                at = slice(t * LANES, (t + 1) * LANES)
                re = jnp.dot(tilts, volume_ref[0, :, at], preferred_element_type=jnp.float32)
                im = jnp.dot(tilts, volume_ref[1, :, at], preferred_element_type=jnp.float32)
                first = (re * cosine - im * sine).astype(jnp.bfloat16)
                second = (re * sine + im * cosine).astype(jnp.bfloat16)
                slices_ref[0, d, :, at] = first
                slices_ref[1, d, :, at] = second
                power += jnp.square(first.astype(jnp.float32)) + jnp.square(second.astype(jnp.float32))
            half_ref[d : d + 1, :] = 0.5 * jnp.sum(power.T, axis=0, keepdims=True)

    return kernel


def wide(ref, rows):
    tiles = ref.shape[1] // ROWS
    pieces = [ref[:, t * ROWS : (t + 1) * ROWS, :].reshape(rows, LANES) for t in range(tiles)]
    return jnp.concatenate(pieces, axis=1)


def inner_kernel(s_ref, own_ref, other_ref, slices_ref, half_ref, out_ref):
    c = s_ref[0]
    groups = own_ref.shape[0]
    rows = groups * ROWS
    own, other = wide(own_ref, rows), wide(other_ref, rows)
    dims = (((1,), (1,)), ((), ()))
    for d in range(slices_ref.shape[1]):
        acc = lax.dot_general(own, slices_ref[c, d], dims, preferred_element_type=jnp.float32)
        acc += lax.dot_general(other, slices_ref[1 - c, d], dims, preferred_element_type=jnp.float32)
        acc = acc - half_ref[d : d + 1, :]
        out_ref[:, d * ROWS : (d + 1) * ROWS, :] = acc.reshape(groups, ROWS, LANES)


def stats_kernel(_, parts_ref, temp_ref, allowed_ref, held_ref, stats_ref):
    inner = parts_ref[0]
    for g in range(1, parts_ref.shape[0]):
        inner = inner + parts_ref[g]
    allowed = allowed_ref[...] > 0.5
    held = jnp.where(allowed, temp_ref[...] * inner / noise_var, masked_fill)
    held_ref[...] = held
    blocks = held.shape[0] // ROWS
    top = jnp.max(held.reshape(blocks, ROWS, LANES), axis=0)
    peak = jnp.broadcast_to(jnp.max(top, axis=1, keepdims=True), (ROWS, LANES))
    full = jnp.concatenate([peak] * blocks, axis=0)
    expo = jnp.where(allowed, jnp.exp(held - full), 0.0)
    total = jnp.sum(jnp.sum(expo.reshape(blocks, ROWS, LANES), axis=0), axis=1, keepdims=True)
    stats_ref[0] = peak
    stats_ref[1] = jnp.broadcast_to(total, (ROWS, LANES))


def posts_kernel(_, held_ref, allowed_ref, mine_ref, theirs_ref, *out_refs):
    peak = jnp.maximum(mine_ref[0], theirs_ref[0])
    total = mine_ref[1] * jnp.exp(mine_ref[0] - peak) + theirs_ref[1] * jnp.exp(theirs_ref[0] - peak)
    for d, out_ref in enumerate(out_refs):
        at = slice(d * ROWS, (d + 1) * ROWS)
        out_ref[...] = jnp.where(allowed_ref[at, :] > 0.5, jnp.exp(held_ref[at, :] - peak) / total, 0.0)


def spread_kernel(s_ref, *refs):
    count = len(refs) - 2
    blocks, (post_ref, copies_ref) = refs[:count], refs[count:]
    x = s_ref[1]
    rounded = jnp.concatenate([b[...] for b in blocks], axis=0).astype(jnp.bfloat16)
    for e, block in enumerate(blocks):
        at = lax.rem(x + count - e, count) * ROWS
        post_ref[pl.ds(pl.multiple_of(at, ROWS), ROWS), :] = block[...]
    for g in range(copies_ref.shape[0]):
        copies_ref[g] = rounded


def final_kernel(s_ref, post_ref, slices_ref, cos_ref, sin_ref, turned_ref, *refs):
    c = s_ref[0]
    images, (sums_ref, mine_ref, theirs_ref) = refs[:-3], refs[-3:]
    own, other = images[: len(images) // 2], images[len(images) // 2 :]
    groups = post_ref.shape[0]
    rows = groups * ROWS
    posts = [
        post_ref[:, e * ROWS : (e + 1) * ROWS, :].reshape(rows, LANES).astype(jnp.float32).T for e in range(len(own))
    ]
    posts = jnp.concatenate(posts, axis=1)
    mass = jnp.sum(posts, axis=1, keepdims=True)
    posts = posts.astype(jnp.bfloat16)
    tiles = own[0].shape[1] // ROWS
    for where, blocks in ((c, own), (1 - c, other)):
        for t in range(tiles):
            piece = jnp.concatenate(
                [b[:, t * ROWS : (t + 1) * ROWS, :].reshape(rows, LANES) for b in blocks], axis=0
            )
            sums_ref[where, :, t * LANES : (t + 1) * LANES] = jnp.dot(
                posts, piece, preferred_element_type=jnp.float32
            )
    cosine, sine = cos_ref[...], sin_ref[...]
    for t in range(tiles):
        at = slice(t * LANES, (t + 1) * LANES)
        first = sums_ref[0, :, at] - mass * slices_ref[0, 0, :, at].astype(jnp.float32)
        second = sums_ref[1, :, at] - mass * slices_ref[1, 0, :, at].astype(jnp.float32)
        grads = []
        for back in (first * cosine + second * sine, second * cosine - first * sine):
            high = back.astype(jnp.bfloat16)
            low = (back - high.astype(jnp.float32)).astype(jnp.bfloat16)
            both = jnp.concatenate([high, low], axis=0)
            grads.append(jnp.dot(turned_ref[...], both, preferred_element_type=jnp.float32) / noise_var)
        mine_ref[:, at] = jnp.where(c == 0, grads[0], grads[1])
        theirs_ref[:, at] = jnp.where(c == 0, grads[1], grads[0]).astype(jnp.bfloat16)


def weave_kernel(_, sums_ref, out_ref):
    width = out_ref.shape[0] // 2
    for part in range(2):
        for t in range(sums_ref.shape[2] // LANES):
            count = min(LANES, width - t * LANES)
            block = sums_ref[part, :, t * LANES : (t + 1) * LANES].T
            out_ref[pl.ds(2 * t * LANES + part, count, stride=2), :] = block[:count]


def join_kernel(s_ref, mine_ref, theirs_ref, out_ref):
    width = out_ref.shape[2]
    real = s_ref[0] == 0
    out_ref[:, 0, :] = jnp.where(real, mine_ref[...], theirs_ref[...])[:, :width]
    out_ref[:, 1, :] = jnp.where(real, theirs_ref[...], mine_ref[...])[:, :width]


def shards(images, shifts, inv_temp, candidates, volume, tilts, azimuth):
    i, x, c = (lax.axis_index(a) for a in ("img", "x", "c"))
    groups, across_x = lax.axis_size("img"), lax.axis_size("x")
    orients, degrees = tilts.shape
    width = volume.shape[2]
    padded = -(-width // LANES) * LANES
    tiles = padded // LANES
    scalars = jnp.stack([c, x, i]).astype(jnp.int32)

    own_temp = lax.dynamic_slice_in_dim(inv_temp, x * ROWS, ROWS, 0)
    cut = cut_images(images, shifts, scalars, width, groups)
    mine = lax.all_to_all(cut.reshape(groups, tiles * ROWS, LANES), "img", 0, 0, tiled=True)
    other = across(mine, "c", 1)

    packed = jnp.concatenate(
        [tilts.T.astype(jnp.float32), azimuth[None, :], jnp.zeros((LANES - degrees - 1, orients), jnp.float32)], axis=0
    )
    gathered = [packed]
    for d in range(1, across_x):
        gathered.append(across(packed, "x", -d))
    gathered = jnp.stack(gathered)
    pad = jnp.pad(jnp.swapaxes(volume, 0, 1), ((0, 0), (0, 0), (0, padded - width)))
    slices, half, cosine, sine = call(
        slices_kernel(width),
        (
            shape((2, across_x, orients, padded), jnp.bfloat16),
            shape((across_x, LANES)),
            shape((orients, LANES)),
            shape((orients, LANES)),
        ),
        scalars,
        gathered,
        pad,
        flops=4 * across_x * orients * degrees * padded,
    )

    partial = call(
        inner_kernel,
        shape((groups, across_x * ROWS, LANES)),
        scalars,
        mine,
        other,
        slices,
        half,
        flops=4 * groups * ROWS * padded * across_x * LANES,
    )
    partial = lax.all_to_all(partial, "img", 0, 0, tiled=True)

    ids = ((x + jnp.arange(across_x)) % across_x * 2 + c)[:, None] * orients + jnp.arange(orients)[None, :]
    allowed = jnp.any(candidates[0][:, None] == ids.reshape(1, -1), axis=0)
    allowed = allowed.astype(jnp.float32)
    allowed = jnp.broadcast_to(allowed.reshape(across_x, 1, orients), (across_x, ROWS, orients)).reshape(-1, orients)
    temp = jnp.broadcast_to(jnp.tile(own_temp, across_x)[:, None], (across_x * ROWS, LANES))
    held, stats = call(
        stats_kernel, (shape((across_x * ROWS, LANES)), shape((2, ROWS, LANES))), scalars, partial, temp, allowed
    )
    blocks = call(
        posts_kernel, [shape((ROWS, LANES))] * across_x, scalars, held, allowed, stats, across(stats, "c", 1)
    )
    blocks = [blocks[0]] + [across(blocks[d], "x", d) for d in range(1, across_x)]
    posteriors, copies = call(
        spread_kernel,
        (shape((across_x * ROWS, LANES)), shape((groups, across_x * ROWS, LANES), jnp.bfloat16)),
        scalars,
        *blocks,
    )
    posts = lax.all_to_all(copies, "img", 0, 0, tiled=True)

    mine_all = [mine]
    for d in range(1, across_x):
        mine_all.append(across(mine, "x", d))
    other_all = [other] + [across(m, "c", 1) for m in mine_all[1:]]
    turned = jnp.concatenate([tilts.T, tilts.T], axis=1)
    sums, grad, theirs = call(
        final_kernel,
        (shape((2, orients, padded)), shape((degrees, padded)), shape((degrees, padded), jnp.bfloat16)),
        scalars,
        posts,
        slices[:, :1],
        cosine,
        sine,
        turned,
        *mine_all,
        *other_all,
        flops=4 * groups * across_x * ROWS * padded * orients,
    )
    woven = call(weave_kernel, shape((2 * width, orients)), scalars, sums)
    weighted_sums = woven.reshape(width, 2, orients)

    theirs = across(theirs, "c", 1)
    grad = (grad + theirs.astype(jnp.float32)).astype(jnp.bfloat16)
    grads = [grad]
    for d in range(1, across_x):
        grads.append(across(grad, "x", d))
    grad = sum(g.astype(jnp.float32) for g in grads)
    theirs = across(grad, "c", 1)
    volume_grad = call(join_kernel, shape((degrees, 2, width)), scalars, grad, theirs)
    return posteriors, weighted_sums, volume_grad


def solution(mesh):
    ori = mesh.shape["ori"]
    finer = Mesh(mesh.devices.reshape(mesh.shape["img"], ori // 2, 2), ("img", "x", "c"))
    return jax.shard_map(
        shards,
        mesh=finer,
        in_specs=(
            P("img", None, None),
            P("img"),
            P("img"),
            P("img", None),
            P(None, None, "img"),
            P(ORI, None),
            P(ORI),
        ),
        out_specs=(P("img", ORI), P("img", None, ORI), P(None, None, "img")),
        check_vma=False,
    )
```

profile of v0, /device:TPU:1, one launch (start us, length us, event | category | flops | bytes accessed | tf_op | source)
XLA Modules:
  0.0 119.4 jit_solution(14166141486110987432)
XLA Ops:
  1.2 3.7 %shard_map.94 = bf16[32,4,8,128]{3,2,1,0:T(8,128)(2,1)} custom-call(s32[3]{0:T(128)} %pad_add_fusion.s_ref._, s32[32]{0:T(128)} %shifts_ref.1, bf16[32,2,16256]{2,1,0:T(2,128)(2,1)} %images_ref.1), custom_call_target="tpu_custom_call" | custom-call | tf_op jit(solution)/shard_map/pallas_call | solution.py:88
  4.9 12.0 %all-to-all-start = ((bf16[32,32,128]{2,1,0:T(8,128)(2,1)}), bf16[32,32,128]{2,1,0:T(8,128)(2,1)S(1)}, u32[]{:S(2)}, u32[]{:S(2)}) async-start(bf16[32,32,128]{2,1,0:T(8,128)(2,1)} %bitcast.23), calls=%async_computation | async-start | bytes 524288 | tf_op jit(solution)/shard_map/all_to_all | solution.py:247
  17.0 9.6 %all-to-all-done.own_ref.refs_0_ = bf16[32,32,128]{2,1,0:T(8,128)(2,1)S(1)} async-done(((bf16[32,32,128]{2,1,0:T(8,128)(2,1)}), bf16[32,32,128]{2,1,0:T(8,128)(2,1)S(1)}, u32[]{:S(2)}, u32[]{:S(2)}) %all-to-all-start) | async-done | bytes 262176 | tf_op jit(solution)/shard_map/all_to_all | solution.py:247
  26.6 3.7 %collective-permute-start = (bf16[32,32,128]{2,1,0:T(8,128)(2,1)S(1)}, bf16[32,32,128]{2,1,0:T(8,128)(2,1)S(1)}, u32[]{:S(2)}, u32[]{:S(2)}) collective-permute-start(bf16[32,32,128]{2,1,0:T(8,128)(2,1)S(1)} %all-to-all-done.own_ref.refs_0_), channel_id=1, source_target_pairs={{0,1},{1,0},{2,3},{3,2},{4,5},{5,4},{6,7},{7,6},{8,9},{9,8},{10,11... | collective-permute-start | bytes 786440 | tf_op jit(solution)/shard_map/ppermute | solution.py:41
  31.7 2.5 %collective-permute-start.2 = (f32[128,128]{1,0:T(8,128)S(1)}, f32[128,128]{1,0:T(8,128)S(1)}, u32[]{:S(2)}, u32[]{:S(2)}) collective-permute-start(f32[128,128]{1,0:T(8,128)S(1)} %get-tuple-element.34), channel_id=1, source_target_pairs={{0,4},{2,6},{4,0},{6,2},{1,5},{3,7},{5,1},{7,3},{8,12},{10,14},{12... | collective-permute-start | bytes 196616 | tf_op jit(solution)/shard_map/ppermute | solution.py:41
  35.4 2.3 %collective-permute-done.2 = f32[128,128]{1,0:T(8,128)S(1)} collective-permute-done((f32[128,128]{1,0:T(8,128)S(1)}, f32[128,128]{1,0:T(8,128)S(1)}, u32[]{:S(2)}, u32[]{:S(2)}) %collective-permute-start.2) | collective-permute-done | bytes 65568 | tf_op jit(solution)/shard_map/ppermute | solution.py:41
  37.8 2.4 %shard_map.95 = (bf16[2,4,128,512]{3,2,1,0:T(8,128)(2,1)S(1)}, f32[4,128]{1,0:T(4,128)S(1)}, f32[128,128]{1,0:T(8,128)S(1)}, f32[128,128]{1,0:T(8,128)S(1)}) custom-call(s32[3]{0:T(128)S(1)} %copy-done.4, f32[4,128,128]{2,1,0:T(8,128)S(1)} %pad_maximum_fusion.packed_ref, bf16[2,64,512]{2,1,0:T(8,128)(2,1)S(1)} %pad.4.volume_ref), custom_call_target="tpu_custom_call" | custom-call | flops 67108864 | bytes 1574912 | tf_op jit(solution)/shard_map/pallas_call | solution.py:25
  40.2 2.0 %shard_map.96 = f32[32,32,128]{2,1,0:T(8,128)} custom-call(s32[3]{0:T(128)S(1)} %copy-done.4, bf16[32,32,128]{2,1,0:T(8,128)(2,1)S(1)} %all-to-all-done.own_ref.refs_0_, bf16[32,32,128]{2,1,0:T(8,128)(2,1)S(1)} %collective-permute-done.other_ref.refs_4_, bf16[2,4,128,512]{3,2,1,0:T(8,128)(2,1)S(1)} %get-tuple-element.18.slices_ref, ...), custom_call_target="tpu_custom_call" | custom-call | flops 268435456 | bytes 2099200 | tf_op jit(solution)/shard_map/pallas_call | solution.py:25
  42.3 4.1 %all-to-all-start.1 = ((f32[32,32,128]{2,1,0:T(8,128)}), f32[32,32,128]{2,1,0:T(8,128)S(1)}, u32[]{:S(2)}, u32[]{:S(2)}) async-start(f32[32,32,128]{2,1,0:T(8,128)} %shard_map.96), calls=%async_computation.1 | async-start | bytes 1048576 | tf_op jit(solution)/shard_map/all_to_all | solution.py:282
  46.9 13.5 %all-to-all-done.1.parts_ref = f32[32,32,128]{2,1,0:T(8,128)S(1)} async-done(((f32[32,32,128]{2,1,0:T(8,128)}), f32[32,32,128]{2,1,0:T(8,128)S(1)}, u32[]{:S(2)}, u32[]{:S(2)}) %all-to-all-start.1) | async-done | bytes 524320 | tf_op jit(solution)/shard_map/all_to_all | solution.py:282
  61.2 4.1 %collective-permute-start.4 = (f32[2,8,128]{2,1,0:T(8,128)S(1)}, f32[2,8,128]{2,1,0:T(8,128)S(1)}, u32[]{:S(2)}, u32[]{:S(2)}) collective-permute-start(f32[2,8,128]{2,1,0:T(8,128)S(1)} %get-tuple-element.21.mine_ref), channel_id=1, source_target_pairs={{0,1},{1,0},{2,3},{3,2},{4,5},{5,4},{6,7},{7,6},{8,9},{9,8},{10,11... | collective-permute-start | bytes 24584 | tf_op jit(solution)/shard_map/ppermute | solution.py:41
  65.3 3.2 %collective-permute-start.9 = (bf16[32,32,128]{2,1,0:T(8,128)(2,1)S(1)}, bf16[32,32,128]{2,1,0:T(8,128)(2,1)S(1)}, u32[]{:S(2)}, u32[]{:S(2)}) collective-permute-start(bf16[32,32,128]{2,1,0:T(8,128)(2,1)S(1)} %all-to-all-done.own_ref.refs_0_), channel_id=1, source_target_pairs={{0,4},{2,6},{4,0},{6,2},{1,5},{3,7},{5,1},{7,3},{8,12},{10,14},{12... | collective-permute-start | bytes 786440 | tf_op jit(solution)/shard_map/ppermute | solution.py:41
  71.1 5.7 %collective-permute-done.5.refs_1_ = f32[8,128]{1,0:T(8,128)S(1)} collective-permute-done((f32[8,128]{1,0:T(8,128)S(1)}, f32[8,128]{1,0:T(8,128)S(1)}, u32[]{:S(2)}, u32[]{:S(2)}) %collective-permute-start.5) | collective-permute-done | bytes 4128 | tf_op jit(solution)/shard_map/ppermute | solution.py:41
  76.9 3.9 %collective-permute-start.7 = (f32[8,128]{1,0:T(8,128)S(1)}, f32[8,128]{1,0:T(8,128)S(1)}, u32[]{:S(2)}, u32[]{:S(2)}) collective-permute-start(f32[8,128]{1,0:T(8,128)S(1)} %get-tuple-element.25), channel_id=1, source_target_pairs={{0,6},{2,0},{4,2},{6,4},{1,7},{3,1},{5,3},{7,5},{8,14},{10,8},{12,... | collective-permute-start | bytes 12296 | tf_op jit(solution)/shard_map/ppermute | solution.py:41
  82.8 5.0 %all-to-all-start.2 = ((bf16[32,32,128]{2,1,0:T(8,128)(2,1)}), bf16[32,32,128]{2,1,0:T(8,128)(2,1)S(1)}, u32[]{:S(2)}, u32[]{:S(2)}) async-start(bf16[32,32,128]{2,1,0:T(8,128)(2,1)} %get-tuple-element.27), calls=%async_computation.2 | async-start | bytes 524288 | tf_op jit(solution)/shard_map/all_to_all | solution.py:302
  87.8 2.2 %collective-permute-start.11 = (bf16[32,32,128]{2,1,0:T(8,128)(2,1)S(1)}, bf16[32,32,128]{2,1,0:T(8,128)(2,1)S(1)}, u32[]{:S(2)}, u32[]{:S(2)}) collective-permute-start(bf16[32,32,128]{2,1,0:T(8,128)(2,1)S(1)} %collective-permute-done.8.refs_1_), channel_id=1, source_target_pairs={{0,1},{1,0},{2,3},{3,2},{4,5},{5,4},{6,7},{7,6},{8,9},{9,8},{10,11... | collective-permute-start | bytes 786440 | tf_op jit(solution)/shard_map/ppermute | solution.py:41
  92.6 4.8 %all-to-all-done.2.post_ref = bf16[32,32,128]{2,1,0:T(8,128)(2,1)S(1)} async-done(((bf16[32,32,128]{2,1,0:T(8,128)(2,1)}), bf16[32,32,128]{2,1,0:T(8,128)(2,1)S(1)}, u32[]{:S(2)}, u32[]{:S(2)}) %all-to-all-start.2) | async-done | bytes 262176 | tf_op jit(solution)/shard_map/all_to_all | solution.py:302
  99.2 1.6 %shard_map.100 = (f32[2,128,512]{2,1,0:T(8,128)S(1)}, f32[64,512]{1,0:T(8,128)S(1)}, bf16[64,512]{1,0:T(8,128)(2,1)S(1)}) custom-call(s32[3]{0:T(128)S(1)} %copy-done.4, bf16[32,32,128]{2,1,0:T(8,128)(2,1)S(1)} %all-to-all-done.2.post_ref, bf16[2,1,128,512]{3,2,1,0:T(8,128)(2,1)S(1)} %slice.3.slices_ref, f32[128,128]{1,0:T(8,128)S(1)} %get-tuple-element.28.cos_ref, ...), custom_call_target="tpu_custom_call" | custom-call | flops 268435456 | bytes 3506176 | tf_op jit(solution)/shard_map/pallas_call | solution.py:25
  100.9 3.8 %collective-permute-start.14 = (bf16[64,512]{1,0:T(8,128)(2,1)S(1)}, bf16[64,512]{1,0:T(8,128)(2,1)S(1)}, u32[]{:S(2)}, u32[]{:S(2)}) collective-permute-start(bf16[64,512]{1,0:T(8,128)(2,1)S(1)} %get-tuple-element.32), channel_id=1, source_target_pairs={{0,1},{1,0},{2,3},{3,2},{4,5},{5,4},{6,7},{7,6},{8,9},{9,8},{10,11... | collective-permute-start | bytes 196616 | tf_op jit(solution)/shard_map/ppermute | solution.py:41
  105.6 3.7 %collective-permute-start.17 = (bf16[64,512]{1,0:T(8,128)(2,1)S(1)}, bf16[64,512]{1,0:T(8,128)(2,1)S(1)}, u32[]{:S(2)}, u32[]{:S(2)}) collective-permute-start(bf16[64,512]{1,0:T(8,128)(2,1)S(1)} %add_convert_fusion), channel_id=1, source_target_pairs={{0,6},{2,0},{4,2},{6,4},{1,7},{3,1},{5,3},{7,5},{8,14},{10,8},{12,... | collective-permute-start | bytes 196616 | tf_op jit(solution)/shard_map/ppermute | solution.py:41
  110.6 3.4 %collective-permute-done.16 = bf16[64,512]{1,0:T(8,128)(2,1)S(1)} collective-permute-done((bf16[64,512]{1,0:T(8,128)(2,1)S(1)}, bf16[64,512]{1,0:T(8,128)(2,1)S(1)}, u32[]{:S(2)}, u32[]{:S(2)}) %collective-permute-start.16) | collective-permute-done | bytes 65568 | tf_op jit(solution)/shard_map/ppermute | solution.py:41
  114.0 1.6 %collective-permute-done.15 = bf16[64,512]{1,0:T(8,128)(2,1)S(1)} collective-permute-done((bf16[64,512]{1,0:T(8,128)(2,1)S(1)}, bf16[64,512]{1,0:T(8,128)(2,1)S(1)}, u32[]{:S(2)}, u32[]{:S(2)}) %collective-permute-start.15) | collective-permute-done | bytes 65568 | tf_op jit(solution)/shard_map/ppermute | solution.py:41
  116.5 1.5 %shard_map.101 = f32[1016,128]{1,0:T(8,128)} custom-call(s32[3]{0:T(128)S(1)} %copy-done.4, f32[2,128,512]{2,1,0:T(8,128)S(1)} %get-tuple-element.30.sums_ref), custom_call_target="tpu_custom_call" | custom-call | bytes 1044480 | tf_op jit(solution)/shard_map/pallas_call | solution.py:25
  118.0 1.3 %shard_map.102 = f32[64,2,508]{2,1,0:T(2,128)} custom-call(s32[3]{0:T(128)S(1)} %copy-done.4, f32[64,512]{1,0:T(8,128)S(1)} %convert_add_fusion.mine_ref, f32[64,512]{1,0:T(8,128)S(1)} %collective-permute-done.18.theirs_ref), custom_call_target="tpu_custom_call" | custom-call | bytes 522240 | tf_op jit(solution)/shard_map/pallas_call | solution.py:25
  (70 shorter events, 16.8 us)
Async XLA Ops:
  0.7 34.7 %copy-start.5 = (bf16[64,2,508]{2,1,0:T(2,128)(2,1)S(1)}, bf16[64,2,508]{2,1,0:T(2,128)(2,1)}, u32[]{:S(2)}) copy-start(bf16[64,2,508]{2,1,0:T(2,128)(2,1)} %param.11) | copy-start | bytes 390148
  1.2 36.5 %copy-start.4 = (s32[3]{0:T(128)S(1)}, s32[3]{0:T(128)}, u32[]{:S(2)}) copy-start(s32[3]{0:T(128)} %pad_add_fusion.s_ref._) | copy-start | bytes 40
  4.9 21.7 %all-to-all-start = ((bf16[32,32,128]{2,1,0:T(8,128)(2,1)}), bf16[32,32,128]{2,1,0:T(8,128)(2,1)S(1)}, u32[]{:S(2)}, u32[]{:S(2)}) async-start(bf16[32,32,128]{2,1,0:T(8,128)(2,1)} %bitcast.23), calls=%async_computation | async-start | bytes 524288 | tf_op jit(solution)/shard_map/all_to_all | solution.py:247
  26.6 13.6 %collective-permute-start = (bf16[32,32,128]{2,1,0:T(8,128)(2,1)S(1)}, bf16[32,32,128]{2,1,0:T(8,128)(2,1)S(1)}, u32[]{:S(2)}, u32[]{:S(2)}) collective-permute-start(bf16[32,32,128]{2,1,0:T(8,128)(2,1)S(1)} %all-to-all-done.own_ref.refs_0_), channel_id=1, source_target_pairs={{0,1},{1,0},{2,3},{3,2},{4,5},{5,4},{6,7},{7,6},{8,9},{9,8},{10,11... | collective-permute-start | bytes 786440 | tf_op jit(solution)/shard_map/ppermute | solution.py:41
  30.4 5.0 %collective-permute-start.3 = (f32[128,128]{1,0:T(8,128)S(1)}, f32[128,128]{1,0:T(8,128)S(1)}, u32[]{:S(2)}, u32[]{:S(2)}) collective-permute-start(f32[128,128]{1,0:T(8,128)S(1)} %get-tuple-element.34), channel_id=1, source_target_pairs={{0,2},{2,4},{4,6},{6,0},{1,3},{3,5},{5,7},{7,1},{8,10},{10,12},{12... | collective-permute-start | bytes 196616 | tf_op jit(solution)/shard_map/ppermute | solution.py:41
  31.7 6.0 %collective-permute-start.2 = (f32[128,128]{1,0:T(8,128)S(1)}, f32[128,128]{1,0:T(8,128)S(1)}, u32[]{:S(2)}, u32[]{:S(2)}) collective-permute-start(f32[128,128]{1,0:T(8,128)S(1)} %get-tuple-element.34), channel_id=1, source_target_pairs={{0,4},{2,6},{4,0},{6,2},{1,5},{3,7},{5,1},{7,3},{8,12},{10,14},{12... | collective-permute-start | bytes 196616 | tf_op jit(solution)/shard_map/ppermute | solution.py:41
  34.2 3.6 %collective-permute-start.1 = (f32[128,128]{1,0:T(8,128)S(1)}, f32[128,128]{1,0:T(8,128)S(1)}, u32[]{:S(2)}, u32[]{:S(2)}) collective-permute-start(f32[128,128]{1,0:T(8,128)S(1)} %get-tuple-element.34), channel_id=1, source_target_pairs={{0,6},{2,0},{4,2},{6,4},{1,7},{3,1},{5,3},{7,5},{8,14},{10,8},{12,... | collective-permute-start | bytes 196616 | tf_op jit(solution)/shard_map/ppermute | solution.py:41
  42.3 18.1 %all-to-all-start.1 = ((f32[32,32,128]{2,1,0:T(8,128)}), f32[32,32,128]{2,1,0:T(8,128)S(1)}, u32[]{:S(2)}, u32[]{:S(2)}) async-start(f32[32,32,128]{2,1,0:T(8,128)} %shard_map.96), calls=%async_computation.1 | async-start | bytes 1048576 | tf_op jit(solution)/shard_map/all_to_all | solution.py:282
  61.2 8.1 %collective-permute-start.4 = (f32[2,8,128]{2,1,0:T(8,128)S(1)}, f32[2,8,128]{2,1,0:T(8,128)S(1)}, u32[]{:S(2)}, u32[]{:S(2)}) collective-permute-start(f32[2,8,128]{2,1,0:T(8,128)S(1)} %get-tuple-element.21.mine_ref), channel_id=1, source_target_pairs={{0,1},{1,0},{2,3},{3,2},{4,5},{5,4},{6,7},{7,6},{8,9},{9,8},{10,11... | collective-permute-start | bytes 24584 | tf_op jit(solution)/shard_map/ppermute | solution.py:41
  65.3 22.5 %collective-permute-start.8 = (bf16[32,32,128]{2,1,0:T(8,128)(2,1)S(1)}, bf16[32,32,128]{2,1,0:T(8,128)(2,1)S(1)}, u32[]{:S(2)}, u32[]{:S(2)}) collective-permute-start(bf16[32,32,128]{2,1,0:T(8,128)(2,1)S(1)} %all-to-all-done.own_ref.refs_0_), channel_id=1, source_target_pairs={{0,2},{2,4},{4,6},{6,0},{1,3},{3,5},{5,7},{7,1},{8,10},{10,12},{12... | collective-permute-start | bytes 786440 | tf_op jit(solution)/shard_map/ppermute | solution.py:41
  65.3 24.7 %collective-permute-start.9 = (bf16[32,32,128]{2,1,0:T(8,128)(2,1)S(1)}, bf16[32,32,128]{2,1,0:T(8,128)(2,1)S(1)}, u32[]{:S(2)}, u32[]{:S(2)}) collective-permute-start(bf16[32,32,128]{2,1,0:T(8,128)(2,1)S(1)} %all-to-all-done.own_ref.refs_0_), channel_id=1, source_target_pairs={{0,4},{2,6},{4,0},{6,2},{1,5},{3,7},{5,1},{7,3},{8,12},{10,14},{12... | collective-permute-start | bytes 786440 | tf_op jit(solution)/shard_map/ppermute | solution.py:41
  68.4 21.7 %collective-permute-start.10 = (bf16[32,32,128]{2,1,0:T(8,128)(2,1)S(1)}, bf16[32,32,128]{2,1,0:T(8,128)(2,1)S(1)}, u32[]{:S(2)}, u32[]{:S(2)}) collective-permute-start(bf16[32,32,128]{2,1,0:T(8,128)(2,1)S(1)} %all-to-all-done.own_ref.refs_0_), channel_id=1, source_target_pairs={{0,6},{2,0},{4,2},{6,4},{1,7},{3,1},{5,3},{7,5},{8,14},{10,8},{12,... | collective-permute-start | bytes 786440 | tf_op jit(solution)/shard_map/ppermute | solution.py:41
  69.9 7.0 %collective-permute-start.5 = (f32[8,128]{1,0:T(8,128)S(1)}, f32[8,128]{1,0:T(8,128)S(1)}, u32[]{:S(2)}, u32[]{:S(2)}) collective-permute-start(f32[8,128]{1,0:T(8,128)S(1)} %get-tuple-element.23), channel_id=1, source_target_pairs={{0,2},{2,4},{4,6},{6,0},{1,3},{3,5},{5,7},{7,1},{8,10},{10,12},{12... | collective-permute-start | bytes 12296 | tf_op jit(solution)/shard_map/ppermute | solution.py:41
  70.5 10.2 %collective-permute-start.6 = (f32[8,128]{1,0:T(8,128)S(1)}, f32[8,128]{1,0:T(8,128)S(1)}, u32[]{:S(2)}, u32[]{:S(2)}) collective-permute-start(f32[8,128]{1,0:T(8,128)S(1)} %get-tuple-element.24), channel_id=1, source_target_pairs={{0,4},{2,6},{4,0},{6,2},{1,5},{3,7},{5,1},{7,3},{8,12},{10,14},{12... | collective-permute-start | bytes 12296 | tf_op jit(solution)/shard_map/ppermute | solution.py:41
  76.9 4.6 %collective-permute-start.7 = (f32[8,128]{1,0:T(8,128)S(1)}, f32[8,128]{1,0:T(8,128)S(1)}, u32[]{:S(2)}, u32[]{:S(2)}) collective-permute-start(f32[8,128]{1,0:T(8,128)S(1)} %get-tuple-element.25), channel_id=1, source_target_pairs={{0,6},{2,0},{4,2},{6,4},{1,7},{3,1},{5,3},{7,5},{8,14},{10,8},{12,... | collective-permute-start | bytes 12296 | tf_op jit(solution)/shard_map/ppermute | solution.py:41
  82.8 14.7 %all-to-all-start.2 = ((bf16[32,32,128]{2,1,0:T(8,128)(2,1)}), bf16[32,32,128]{2,1,0:T(8,128)(2,1)S(1)}, u32[]{:S(2)}, u32[]{:S(2)}) async-start(bf16[32,32,128]{2,1,0:T(8,128)(2,1)} %get-tuple-element.27), calls=%async_computation.2 | async-start | bytes 524288 | tf_op jit(solution)/shard_map/all_to_all | solution.py:302
  87.8 3.4 %collective-permute-start.11 = (bf16[32,32,128]{2,1,0:T(8,128)(2,1)S(1)}, bf16[32,32,128]{2,1,0:T(8,128)(2,1)S(1)}, u32[]{:S(2)}, u32[]{:S(2)}) collective-permute-start(bf16[32,32,128]{2,1,0:T(8,128)(2,1)S(1)} %collective-permute-done.8.refs_1_), channel_id=1, source_target_pairs={{0,1},{1,0},{2,3},{3,2},{4,5},{5,4},{6,7},{7,6},{8,9},{9,8},{10,11... | collective-permute-start | bytes 786440 | tf_op jit(solution)/shard_map/ppermute | solution.py:41
  90.0 1.5 %collective-permute-start.12 = (bf16[32,32,128]{2,1,0:T(8,128)(2,1)S(1)}, bf16[32,32,128]{2,1,0:T(8,128)(2,1)S(1)}, u32[]{:S(2)}, u32[]{:S(2)}) collective-permute-start(bf16[32,32,128]{2,1,0:T(8,128)(2,1)S(1)} %collective-permute-done.9.refs_2_), channel_id=1, source_target_pairs={{0,1},{1,0},{2,3},{3,2},{4,5},{5,4},{6,7},{7,6},{8,9},{9,8},{10,11... | collective-permute-start | bytes 786440 | tf_op jit(solution)/shard_map/ppermute | solution.py:41
  90.1 1.8 %collective-permute-start.13 = (bf16[32,32,128]{2,1,0:T(8,128)(2,1)S(1)}, bf16[32,32,128]{2,1,0:T(8,128)(2,1)S(1)}, u32[]{:S(2)}, u32[]{:S(2)}) collective-permute-start(bf16[32,32,128]{2,1,0:T(8,128)(2,1)S(1)} %collective-permute-done.10.refs_3_), channel_id=1, source_target_pairs={{0,1},{1,0},{2,3},{3,2},{4,5},{5,4},{6,7},{7,6},{8,9},{9,8},{10,11... | collective-permute-start | bytes 786440 | tf_op jit(solution)/shard_map/ppermute | solution.py:41
  100.9 4.7 %collective-permute-start.14 = (bf16[64,512]{1,0:T(8,128)(2,1)S(1)}, bf16[64,512]{1,0:T(8,128)(2,1)S(1)}, u32[]{:S(2)}, u32[]{:S(2)}) collective-permute-start(bf16[64,512]{1,0:T(8,128)(2,1)S(1)} %get-tuple-element.32), channel_id=1, source_target_pairs={{0,1},{1,0},{2,3},{3,2},{4,5},{5,4},{6,7},{7,6},{8,9},{9,8},{10,11... | collective-permute-start | bytes 196616 | tf_op jit(solution)/shard_map/ppermute | solution.py:41
  105.6 5.0 %collective-permute-start.17 = (bf16[64,512]{1,0:T(8,128)(2,1)S(1)}, bf16[64,512]{1,0:T(8,128)(2,1)S(1)}, u32[]{:S(2)}, u32[]{:S(2)}) collective-permute-start(bf16[64,512]{1,0:T(8,128)(2,1)S(1)} %add_convert_fusion), channel_id=1, source_target_pairs={{0,6},{2,0},{4,2},{6,4},{1,7},{3,1},{5,3},{7,5},{8,14},{10,8},{12,... | collective-permute-start | bytes 196616 | tf_op jit(solution)/shard_map/ppermute | solution.py:41
  109.3 4.7 %collective-permute-start.16 = (bf16[64,512]{1,0:T(8,128)(2,1)S(1)}, bf16[64,512]{1,0:T(8,128)(2,1)S(1)}, u32[]{:S(2)}, u32[]{:S(2)}) collective-permute-start(bf16[64,512]{1,0:T(8,128)(2,1)S(1)} %add_convert_fusion), channel_id=1, source_target_pairs={{0,4},{2,6},{4,0},{6,2},{1,5},{3,7},{5,1},{7,3},{8,12},{10,14},{12... | collective-permute-start | bytes 196616 | tf_op jit(solution)/shard_map/ppermute | solution.py:41
  109.3 6.3 %collective-permute-start.15 = (bf16[64,512]{1,0:T(8,128)(2,1)S(1)}, bf16[64,512]{1,0:T(8,128)(2,1)S(1)}, u32[]{:S(2)}, u32[]{:S(2)}) collective-permute-start(bf16[64,512]{1,0:T(8,128)(2,1)S(1)} %add_convert_fusion), channel_id=1, source_target_pairs={{0,2},{2,4},{4,6},{6,0},{1,3},{3,5},{5,7},{7,1},{8,10},{10,12},{12... | collective-permute-start | bytes 196616 | tf_op jit(solution)/shard_map/ppermute | solution.py:41
  115.6 2.4 %collective-permute-start.18 = (f32[64,512]{1,0:T(8,128)S(1)}, f32[64,512]{1,0:T(8,128)S(1)}, u32[]{:S(2)}, u32[]{:S(2)}) collective-permute-start(f32[64,512]{1,0:T(8,128)S(1)} %convert_add_fusion.mine_ref), channel_id=1, source_target_pairs={{0,1},{1,0},{2,3},{3,2},{4,5},{5,4},{6,7},{7,6},{8,9},{9,8},{10,11... | collective-permute-start | bytes 393224 | tf_op jit(solution)/shard_map/ppermute | solution.py:41
  (8 other events, 73.0 us)
where the time goes:
time: 120 us; the launch traced here: 119 us
  starting transfers between devices  54.8 us (46%)
  waiting for transfers between devices  44.6 us (37%)
  Pallas kernels  15.1 us (13%)
  local copies, waits for them, and re-layouts  2.89 us (2%)
    ppermute x19, starting transfers between devices, across(): lax.ppermute(x, axis, [(s, (s + step) % count) for s in range(count)])  33.6 us
    ppermute x19, waiting for transfers between devices, across(): lax.ppermute(x, axis, [(s, (s + step) % count) for s in range(count)])  16.8 us
    all_to_all x1, waiting for transfers between devices, shards(): partial = lax.all_to_all(partial, 'img', 0, 0, tiled=True)  13.5 us
    all_to_all x1, starting transfers between devices, shards(): lax.all_to_all(cut.reshape(groups, tiles * ROWS, LANES), 'img', 0, 0, til...  12 us
    pallas_call x8, Pallas kernels, call(): pl.pallas_call(kernel, out_shape=out_shape, in_specs=specs, out_specs=out...  11.5 us
    all_to_all x1, waiting for transfers between devices, shards(): lax.all_to_all(cut.reshape(groups, tiles * ROWS, LANES), 'img', 0, 0, til...  9.59 us
    all_to_all x1, starting transfers between devices, shards(): posts = lax.all_to_all(copies, 'img', 0, 0, tiled=True)  5.02 us
    all_to_all x1, waiting for transfers between devices, shards(): posts = lax.all_to_all(copies, 'img', 0, 0, tiled=True)  4.81 us
  transfers between devices with their start and end apart: 22, of which 13 were waited for; matrix products, arithmetic and copies ran while one was open for 1% of the time, Pallas kernels for 5%

commit v1 on v0

--- a/solution.py
+++ b/solution.py
@@ -13,13 +13,15 @@
 LANES = 128
 ROWS = 8
 ORDERS = 64
+CUTS = 4
 noise_var = 128.0
 masked_fill = -1e30
 ORI = ("x", "c")
 
 
 def call(kernel, out_shape, scalars, *args, flops=0):
-    specs = [pl.BlockSpec(memory_space=pltpu.SMEM)] + [pl.BlockSpec(memory_space=pltpu.VMEM)] * len(args)
+    scalars = scalars if isinstance(scalars, tuple) else (scalars,)
+    specs = [pl.BlockSpec(memory_space=pltpu.SMEM)] * len(scalars) + [pl.BlockSpec(memory_space=pltpu.VMEM)] * len(args)
     outs = jax.tree.map(lambda _: pl.BlockSpec(memory_space=pltpu.VMEM), out_shape)
     moved = sum(a.size * a.dtype.itemsize for a in (*args, *jax.tree.leaves(out_shape)))
     return pl.pallas_call(
@@ -29,16 +31,15 @@
         out_specs=outs,
         compiler_params=pltpu.CompilerParams(vmem_limit_bytes=8 * 2**20),
         cost_estimate=pl.CostEstimate(flops=flops, transcendentals=0, bytes_accessed=moved),
-    )(scalars, *args)
+    )(*scalars, *args)
 
 
 def shape(dims, dtype=jnp.float32):
     return jax.ShapeDtypeStruct(dims, dtype)
 
 
-def across(x, axis, step):
-    count = lax.axis_size(axis)
-    return lax.ppermute(x, axis, [(s, (s + step) % count) for s in range(count)])
+def across(x, axis, turn):
+    return lax.ppermute(x, axis, [(s, s ^ turn) for s in range(lax.axis_size(axis))])
 
 
 def orders(start):
@@ -49,8 +50,19 @@
 def rotate_and_cut(width, parts):
     tiles = -(-width // LANES)
 
-    def kernel(s_ref, shifts_ref, images_ref, out_ref):
-        c, x = s_ref[0], s_ref[1]
+    def kernel(shifts_ref, images_ref, out_ref, block, sems):
+        c, x = lax.axis_index("c"), lax.axis_index("x")
+        whole = images_ref.shape[2] // LANES
+        bounds = [whole * k // CUTS for k in range(CUTS + 1)]
+        copies = []
+        for k in range(CUTS):
+            at = slice(bounds[k] * LANES, bounds[k + 1] * LANES)
+            copies.append(
+                pltpu.make_async_copy(
+                    images_ref.at[pl.ds(x * ROWS, ROWS), :, at], block.at[:, :, at], sems.at[k]
+                )
+            )
+            copies[-1].start()
         row = lax.broadcasted_iota(jnp.int32, (ROWS, LANES), 0)
         phase = jnp.zeros((ROWS, LANES), jnp.float32)
         for n in range(ROWS):
@@ -60,55 +72,68 @@
         a = jnp.where(c == 0, cosine, sine)
         b = jnp.where(c == 0, -sine, cosine)
         lane = lax.broadcasted_iota(jnp.int32, (ROWS, LANES), 1)
-        whole = images_ref.shape[2] // LANES
-        turned = []
-        for k in range(whole):
-            at = slice(k * LANES, (k + 1) * LANES)
-            both = images_ref[:, :, at].astype(jnp.float32)
-            turned.append(both[:, 0, :] * a + both[:, 1, :] * b)
-        for part in range(parts):
-            shift = (part * width) % LANES
-            for t in range(tiles):
-                first = part * width // LANES + t
-                one = turned[first]
-                if shift:
-                    two = turned[min(first + 1, whole - 1)]
-                    one = jnp.where(lane < shift, two, one)
-                    one = pltpu.roll(one, LANES - shift, 1)
-                left = width - t * LANES
-                if left < LANES:
-                    one = jnp.where(lane < left, one, 0.0)
-                out_ref[part, t] = one.astype(jnp.bfloat16)
+        turned, part = [], 0
+        for k in range(CUTS):
+            copies[k].wait()
+            for tile in range(bounds[k], bounds[k + 1]):
+                both = block[:, :, tile * LANES : (tile + 1) * LANES].astype(jnp.float32)
+                turned.append(both[:, 0, :] * a + both[:, 1, :] * b)
+            while part < parts and (part + 1) * width <= len(turned) * LANES:
+                shift = (part * width) % LANES
+                for t in range(tiles):
+                    first = part * width // LANES + t
+                    one = turned[first]
+                    if shift:
+                        two = turned[min(first + 1, len(turned) - 1)]
+                        one = jnp.where(lane < shift, two, one)
+                        one = pltpu.roll(one, LANES - shift, 1)
+                    left = width - t * LANES
+                    if left < LANES:
+                        one = jnp.where(lane < left, one, 0.0)
+                    out_ref[part, t] = one.astype(jnp.bfloat16)
+                part += 1
 
     return kernel
 
 
-def cut_images(images, shifts, scalars, width, parts):
+def cut_images(images, shifts, width, parts):
     tiles = -(-width // LANES)
     return pl.pallas_call(
         rotate_and_cut(width, parts),
         out_shape=shape((parts, tiles, ROWS, LANES), jnp.bfloat16),
-        grid_spec=pltpu.PrefetchScalarGridSpec(
-            num_scalar_prefetch=2,
-            grid=(1,),
-            in_specs=[pl.BlockSpec((ROWS, 2, images.shape[2]), lambda g, s, n: (s[1], 0, 0))],
-            out_specs=pl.BlockSpec((parts, tiles, ROWS, LANES), lambda g, s, n: (0, 0, 0, 0)),
-        ),
+        in_specs=[pl.BlockSpec(memory_space=pltpu.SMEM), pl.BlockSpec(memory_space=pl.ANY)],
+        out_specs=pl.BlockSpec(memory_space=pltpu.VMEM),
+        scratch_shapes=[pltpu.VMEM((ROWS, 2, images.shape[2]), jnp.bfloat16), pltpu.SemaphoreType.DMA((CUTS,))],
         compiler_params=pltpu.CompilerParams(vmem_limit_bytes=60 * 2**20),
-    )(scalars, shifts, images)
+    )(shifts, images)
 
 
 def slices_kernel(width):
-    def kernel(s_ref, packed_ref, volume_ref, slices_ref, half_ref, cos_ref, sin_ref):
+    def kernel(s_ref, temp_ref, listed_ref, packed_ref, volume_ref, slices_ref, half_ref, temps_ref, allowed_ref):
+        c, x = s_ref[0], s_ref[1]
         degrees = volume_ref.shape[1]
+        row = lax.broadcasted_iota(jnp.int32, (ROWS, LANES), 0)
+        temps = jnp.zeros((ROWS, LANES), jnp.float32)
+        for n in range(ROWS):
+            temps = jnp.where(row == n, temp_ref[x * ROWS + n], temps)
+        listed = [
+            jnp.broadcast_to(listed_ref[k : k + 1, :].astype(jnp.float32), (LANES, LANES)).T
+            for k in range(listed_ref.shape[0])
+        ]
+        lane = lax.broadcasted_iota(jnp.int32, (1, LANES), 1)
         order = orders(s_ref[2] * width)
         for d in range(packed_ref.shape[0]):
+            ids = (((x ^ d) * 2 + c) * LANES + lane).astype(jnp.float32)
+            found = jnp.zeros((LANES, LANES), jnp.float32)
+            for one in listed:
+                found = jnp.where(one == ids, 1.0, found)
+            allowed_ref[d * ROWS : (d + 1) * ROWS, :] = jnp.broadcast_to(
+                jnp.max(found, axis=0, keepdims=True), (ROWS, LANES)
+            )
+            temps_ref[d * ROWS : (d + 1) * ROWS, :] = temps
             block = packed_ref[d].T
             angles = jnp.broadcast_to(block[:, degrees : degrees + 1], block.shape) * order
             cosine, sine = jnp.cos(angles), jnp.sin(angles)
-            if d == 0:
-                cos_ref[...] = cosine
-                sin_ref[...] = sine
             tilts = block[:, :degrees].astype(jnp.bfloat16)
             power = jnp.zeros_like(block)
             for t in range(volume_ref.shape[2] // LANES):
@@ -121,6 +146,15 @@
                 slices_ref[1, d, :, at] = second
                 power += jnp.square(first.astype(jnp.float32)) + jnp.square(second.astype(jnp.float32))
             half_ref[d : d + 1, :] = 0.5 * jnp.sum(power.T, axis=0, keepdims=True)
+
+    return kernel
+
+
+def turns_kernel(width):
+    def kernel(s_ref, azimuth_ref, turn_ref):
+        angles = jnp.broadcast_to(azimuth_ref[...], (LANES, LANES)).T * orders(s_ref[2] * width)
+        turn_ref[0] = jnp.cos(angles)
+        turn_ref[1] = jnp.sin(angles)
 
     return kernel
 
@@ -161,34 +195,25 @@
     stats_ref[1] = jnp.broadcast_to(total, (ROWS, LANES))
 
 
-def posts_kernel(_, held_ref, allowed_ref, mine_ref, theirs_ref, *out_refs):
+def posts_kernel(s_ref, held_ref, allowed_ref, mine_ref, theirs_ref, out_ref):
     peak = jnp.maximum(mine_ref[0], theirs_ref[0])
     total = mine_ref[1] * jnp.exp(mine_ref[0] - peak) + theirs_ref[1] * jnp.exp(theirs_ref[0] - peak)
-    for d, out_ref in enumerate(out_refs):
+    for d in range(out_ref.shape[1]):
         at = slice(d * ROWS, (d + 1) * ROWS)
-        out_ref[...] = jnp.where(allowed_ref[at, :] > 0.5, jnp.exp(held_ref[at, :] - peak) / total, 0.0)
-
-
-def spread_kernel(s_ref, *refs):
-    count = len(refs) - 2
-    blocks, (post_ref, copies_ref) = refs[:count], refs[count:]
-    x = s_ref[1]
-    rounded = jnp.concatenate([b[...] for b in blocks], axis=0).astype(jnp.bfloat16)
-    for e, block in enumerate(blocks):
-        at = lax.rem(x + count - e, count) * ROWS
-        post_ref[pl.ds(pl.multiple_of(at, ROWS), ROWS), :] = block[...]
-    for g in range(copies_ref.shape[0]):
-        copies_ref[g] = rounded
-
-
-def final_kernel(s_ref, post_ref, slices_ref, cos_ref, sin_ref, turned_ref, *refs):
+        posts = jnp.where(allowed_ref[at, :] > 0.5, jnp.exp(held_ref[at, :] - peak) / total, 0.0)
+        posts = posts.astype(jnp.bfloat16)
+        for g in range(out_ref.shape[0]):
+            out_ref[g, s_ref[1] ^ d] = posts
+
+
+def final_kernel(s_ref, post_ref, slices_ref, turn_ref, turned_ref, *refs):
     c = s_ref[0]
     images, (sums_ref, mine_ref, theirs_ref) = refs[:-3], refs[-3:]
     own, other = images[: len(images) // 2], images[len(images) // 2 :]
     groups = post_ref.shape[0]
     rows = groups * ROWS
     posts = [
-        post_ref[:, e * ROWS : (e + 1) * ROWS, :].reshape(rows, LANES).astype(jnp.float32).T for e in range(len(own))
+        post_ref[:, s_ref[1] ^ e].reshape(rows, LANES).astype(jnp.float32).T for e in range(len(own))
     ]
     posts = jnp.concatenate(posts, axis=1)
     mass = jnp.sum(posts, axis=1, keepdims=True)
@@ -202,7 +227,7 @@
             sums_ref[where, :, t * LANES : (t + 1) * LANES] = jnp.dot(
                 posts, piece, preferred_element_type=jnp.float32
             )
-    cosine, sine = cos_ref[...], sin_ref[...]
+    cosine, sine = turn_ref[0], turn_ref[1]
     for t in range(tiles):
         at = slice(t * LANES, (t + 1) * LANES)
         first = sums_ref[0, :, at] - mass * slices_ref[0, 0, :, at].astype(jnp.float32)
@@ -217,7 +242,8 @@
         theirs_ref[:, at] = jnp.where(c == 0, grads[1], grads[0]).astype(jnp.bfloat16)
 
 
-def weave_kernel(_, sums_ref, out_ref):
+def weave_kernel(s_ref, sums_ref, post_ref, out_ref, own_ref):
+    own_ref[...] = post_ref[s_ref[2]].astype(jnp.float32)
     width = out_ref.shape[0] // 2
     for part in range(2):
         for t in range(sums_ref.shape[2] // LANES):
@@ -242,8 +268,7 @@
     tiles = padded // LANES
     scalars = jnp.stack([c, x, i]).astype(jnp.int32)
 
-    own_temp = lax.dynamic_slice_in_dim(inv_temp, x * ROWS, ROWS, 0)
-    cut = cut_images(images, shifts, scalars, width, groups)
+    cut = cut_images(images, shifts, width, groups)
     mine = lax.all_to_all(cut.reshape(groups, tiles * ROWS, LANES), "img", 0, 0, tiled=True)
     other = across(mine, "c", 1)
 
@@ -252,18 +277,19 @@
     )
     gathered = [packed]
     for d in range(1, across_x):
-        gathered.append(across(packed, "x", -d))
+        gathered.append(across(packed, "x", d))
     gathered = jnp.stack(gathered)
     pad = jnp.pad(jnp.swapaxes(volume, 0, 1), ((0, 0), (0, 0), (0, padded - width)))
-    slices, half, cosine, sine = call(
+    slices, half, temps, allowed = call(
         slices_kernel(width),
         (
             shape((2, across_x, orients, padded), jnp.bfloat16),
             shape((across_x, LANES)),
-            shape((orients, LANES)),
-            shape((orients, LANES)),
+            shape((across_x * ROWS, LANES)),
+            shape((across_x * ROWS, LANES)),
         ),
-        scalars,
+        (scalars, inv_temp),
+        candidates.reshape(-1, LANES),
         gathered,
         pad,
         flops=4 * across_x * orients * degrees * padded,
@@ -281,45 +307,47 @@
     )
     partial = lax.all_to_all(partial, "img", 0, 0, tiled=True)
 
-    ids = ((x + jnp.arange(across_x)) % across_x * 2 + c)[:, None] * orients + jnp.arange(orients)[None, :]
-    allowed = jnp.any(candidates[0][:, None] == ids.reshape(1, -1), axis=0)
-    allowed = allowed.astype(jnp.float32)
-    allowed = jnp.broadcast_to(allowed.reshape(across_x, 1, orients), (across_x, ROWS, orients)).reshape(-1, orients)
-    temp = jnp.broadcast_to(jnp.tile(own_temp, across_x)[:, None], (across_x * ROWS, LANES))
     held, stats = call(
-        stats_kernel, (shape((across_x * ROWS, LANES)), shape((2, ROWS, LANES))), scalars, partial, temp, allowed
-    )
-    blocks = call(
-        posts_kernel, [shape((ROWS, LANES))] * across_x, scalars, held, allowed, stats, across(stats, "c", 1)
-    )
-    blocks = [blocks[0]] + [across(blocks[d], "x", d) for d in range(1, across_x)]
-    posteriors, copies = call(
-        spread_kernel,
-        (shape((across_x * ROWS, LANES)), shape((groups, across_x * ROWS, LANES), jnp.bfloat16)),
+        stats_kernel, (shape((across_x * ROWS, LANES)), shape((2, ROWS, LANES))), scalars, partial, temps, allowed
+    )
+    copies = call(
+        posts_kernel,
+        shape((groups, across_x, ROWS, LANES), jnp.bfloat16),
         scalars,
-        *blocks,
-    )
-    posts = lax.all_to_all(copies, "img", 0, 0, tiled=True)
+        held,
+        allowed,
+        stats,
+        across(stats, "c", 1),
+    )
+    copies = copies.reshape(groups * across_x, ROWS, LANES)
+    posts = lax.all_to_all(copies, ("img", "x"), 0, 0, tiled=True)
+    posts = posts.reshape(groups, across_x, ROWS, LANES)
 
     mine_all = [mine]
     for d in range(1, across_x):
         mine_all.append(across(mine, "x", d))
     other_all = [other] + [across(m, "c", 1) for m in mine_all[1:]]
     turned = jnp.concatenate([tilts.T, tilts.T], axis=1)
+    turns = call(turns_kernel(width), shape((2, orients, LANES)), scalars, azimuth[None, :])
     sums, grad, theirs = call(
         final_kernel,
         (shape((2, orients, padded)), shape((degrees, padded)), shape((degrees, padded), jnp.bfloat16)),
         scalars,
         posts,
         slices[:, :1],
-        cosine,
-        sine,
+        turns,
         turned,
         *mine_all,
         *other_all,
         flops=4 * groups * across_x * ROWS * padded * orients,
     )
-    woven = call(weave_kernel, shape((2 * width, orients)), scalars, sums)
+    woven, posteriors = call(
+        weave_kernel,
+        (shape((2 * width, orients)), shape((across_x * ROWS, LANES))),
+        scalars,
+        sums,
+        posts.reshape(groups, across_x * ROWS, LANES),
+    )
     weighted_sums = woven.reshape(width, 2, orients)
 
     theirs = across(theirs, "c", 1)

time: 120 us -> 109 us (0.908)
  waiting for transfers between devices: 44.6 us -> 23.3 us
  blocking collectives: 0 us -> 16.9 us
  starting transfers between devices: 54.8 us -> 49.4 us
    all_to_all x0 -> x1, blocking collectives: none -> 16.9 us  [shards(): partial = lax.all_to_all(partial, 'img', 0, 0, tiled=True)]
    all_to_all x2 -> x1, waiting for transfers between devices: 18.3 us -> 6.96 us  [shards(): posts = lax.all_to_all(copies, ('img', 'x'), 0, 0, tiled=True)]
    ppermute x19 -> x16, waiting for transfers between devices: 16.8 us -> 6.76 us  [across(): lax.ppermute(x, axis, [(s, s ^ turn) for s in range(lax.axis_size(axis))])]
    ppermute x19 -> x16, starting transfers between devices: 33.6 us -> 28.6 us  [across(): lax.ppermute(x, axis, [(s, s ^ turn) for s in range(lax.axis_size(axis))])]
    all_to_all x2 -> x1, starting transfers between devices: 9.15 us -> 8.76 us  [shards(): posts = lax.all_to_all(copies, ('img', 'x'), 0, 0, tiled=True)]
    unnamed x21 -> x17, local copies, waits for them, and re-layouts: 2.54 us -> 2.44 us
  transfers between devices with their start and end apart: 22 -> 18, of which waited for: 13 -> 8; matrix products, arithmetic and copies ran while one was open for 1% -> 1% of each run, Pallas kernels for 5% -> 6%
where the time goes in v1:
time: 109 us
  starting transfers between devices  49.4 us (45%)
  waiting for transfers between devices  23.3 us (21%)
  blocking collectives  16.9 us (16%)
  Pallas kernels  14.7 us (13%)
  local copies, waits for them, and re-layouts  2.55 us (2%)
    ppermute x16, starting transfers between devices, across(): lax.ppermute(x, axis, [(s, s ^ turn) for s in range(lax.axis_size(axis))])  28.6 us
    all_to_all x1, blocking collectives, shards(): partial = lax.all_to_all(partial, 'img', 0, 0, tiled=True)  16.9 us
    all_to_all x1, starting transfers between devices, shards(): lax.all_to_all(cut.reshape(groups, tiles * ROWS, LANES), 'img', 0, 0, til...  12 us
    pallas_call x8, Pallas kernels, call(): pl.pallas_call(kernel, out_shape=out_shape, in_specs=specs, out_specs=out...  11 us
    all_to_all x1, waiting for transfers between devices, shards(): lax.all_to_all(cut.reshape(groups, tiles * ROWS, LANES), 'img', 0, 0, til...  9.59 us
    all_to_all x1, starting transfers between devices, shards(): posts = lax.all_to_all(copies, ('img', 'x'), 0, 0, tiled=True)  8.76 us
    all_to_all x1, waiting for transfers between devices, shards(): posts = lax.all_to_all(copies, ('img', 'x'), 0, 0, tiled=True)  6.96 us
    ppermute x16, waiting for transfers between devices, across(): lax.ppermute(x, axis, [(s, s ^ turn) for s in range(lax.axis_size(axis))])  6.76 us
  transfers between devices with their start and end apart: 18, of which 8 were waited for; matrix products, arithmetic and copies ran while one was open for 1% of the time, Pallas kernels for 6%

profile of v1, /device:TPU:1, one launch (start us, length us, event | category | flops | bytes accessed | tf_op | source)
XLA Modules:
  0.0 108.6 jit_solution(6231969008877934986)
XLA Ops:
  0.7 3.7 %shard_map.94 = bf16[32,4,8,128]{3,2,1,0:T(8,128)(2,1)} custom-call(s32[32]{0:T(128)} %shifts_ref.1, bf16[32,2,16256]{2,1,0:T(2,128)(2,1)} %images_ref.1), custom_call_target="tpu_custom_call" | custom-call | tf_op jit(solution)/shard_map/pallas_call | solution.py:101
  4.4 12.0 %all-to-all-start = ((bf16[32,32,128]{2,1,0:T(8,128)(2,1)}), bf16[32,32,128]{2,1,0:T(8,128)(2,1)S(1)}, u32[]{:S(2)}, u32[]{:S(2)}) async-start(bf16[32,32,128]{2,1,0:T(8,128)(2,1)} %bitcast.25), calls=%async_computation | async-start | bytes 524288 | tf_op jit(solution)/shard_map/all_to_all | solution.py:272
  16.5 9.6 %all-to-all-done.own_ref.refs_0_ = bf16[32,32,128]{2,1,0:T(8,128)(2,1)S(1)} async-done(((bf16[32,32,128]{2,1,0:T(8,128)(2,1)}), bf16[32,32,128]{2,1,0:T(8,128)(2,1)S(1)}, u32[]{:S(2)}, u32[]{:S(2)}) %all-to-all-start) | async-done | bytes 262176 | tf_op jit(solution)/shard_map/all_to_all | solution.py:272
  26.1 3.7 %collective-permute-start = (bf16[32,32,128]{2,1,0:T(8,128)(2,1)S(1)}, bf16[32,32,128]{2,1,0:T(8,128)(2,1)S(1)}, u32[]{:S(2)}, u32[]{:S(2)}) collective-permute-start(bf16[32,32,128]{2,1,0:T(8,128)(2,1)S(1)} %all-to-all-done.own_ref.refs_0_), channel_id=1, source_target_pairs={{0,1},{1,0},{2,3},{3,2},{4,5},{5,4},{6,7},{7,6},{8,9},{9,8},{10,11... | collective-permute-start | bytes 786440 | tf_op jit(solution)/shard_map/ppermute | solution.py:42
  29.9 2.6 %collective-permute-start.3 = (f32[128,128]{1,0:T(8,128)S(1)}, f32[128,128]{1,0:T(8,128)S(1)}, u32[]{:S(2)}, u32[]{:S(2)}) collective-permute-start(f32[128,128]{1,0:T(8,128)S(1)} %get-tuple-element.26), channel_id=1, source_target_pairs={{0,6},{2,4},{4,2},{6,0},{1,7},{3,5},{5,3},{7,1},{8,14},{10,12},{12... | collective-permute-start | bytes 196616 | tf_op jit(solution)/shard_map/ppermute | solution.py:42
  32.5 1.4 %collective-permute-start.2 = (f32[128,128]{1,0:T(8,128)S(1)}, f32[128,128]{1,0:T(8,128)S(1)}, u32[]{:S(2)}, u32[]{:S(2)}) collective-permute-start(f32[128,128]{1,0:T(8,128)S(1)} %get-tuple-element.26), channel_id=1, source_target_pairs={{0,4},{2,6},{4,0},{6,2},{1,5},{3,7},{5,1},{7,3},{8,12},{10,14},{12... | collective-permute-start | bytes 196616 | tf_op jit(solution)/shard_map/ppermute | solution.py:42
  35.6 1.5 %collective-permute-done.2 = f32[128,128]{1,0:T(8,128)S(1)} collective-permute-done((f32[128,128]{1,0:T(8,128)S(1)}, f32[128,128]{1,0:T(8,128)S(1)}, u32[]{:S(2)}, u32[]{:S(2)}) %collective-permute-start.2) | collective-permute-done | bytes 65568 | tf_op jit(solution)/shard_map/ppermute | solution.py:42
  37.2 2.4 %shard_map.95 = (bf16[2,4,128,512]{3,2,1,0:T(8,128)(2,1)S(1)}, f32[4,128]{1,0:T(4,128)S(1)}, f32[32,128]{1,0:T(8,128)S(1)}, f32[32,128]{1,0:T(8,128)S(1)}) custom-call(s32[3]{0:T(128)S(1)} %pad_add_fusion.s_ref._, f32[32]{0:T(128)S(1)} %copy-done.5, s32[4,128]{1,0:T(4,128)S(1)} %bitcast.22, f32[4,128,128]{2,1,0:T(8,128)S(1)} %pad_maximum_fusion.packed_ref, ...), custom_call_target="tpu_custom_call" | custom-call | flops 67108864 | bytes 1478656 | tf_op jit(solution)/shard_map/pallas_call | solution.py:27
  40.9 16.9 %all_to_all.15.parts_ref = f32[32,32,128]{2,1,0:T(8,128)S(1)} all-to-all(f32[32,32,128]{2,1,0:T(8,128)S(1)} %shard_map.96), channel_id=1, replica_groups=mesh['img'=32,'x'=4,'c'=2] {'img'}, dimensions={0} | all-to-all | bytes 1048576 | tf_op jit(solution)/shard_map/all_to_all | solution.py:308
  58.6 5.2 %collective-permute-start.4 = (f32[2,8,128]{2,1,0:T(8,128)S(1)}, f32[2,8,128]{2,1,0:T(8,128)S(1)}, u32[]{:S(2)}, u32[]{:S(2)}) collective-permute-start(f32[2,8,128]{2,1,0:T(8,128)S(1)} %get-tuple-element.19.mine_ref), channel_id=1, source_target_pairs={{0,1},{1,0},{2,3},{3,2},{4,5},{5,4},{6,7},{7,6},{8,9},{9,8},{10,11... | collective-permute-start | bytes 24584 | tf_op jit(solution)/shard_map/ppermute | solution.py:42
  63.7 2.3 %collective-permute-start.7 = (bf16[32,32,128]{2,1,0:T(8,128)(2,1)S(1)}, bf16[32,32,128]{2,1,0:T(8,128)(2,1)S(1)}, u32[]{:S(2)}, u32[]{:S(2)}) collective-permute-start(bf16[32,32,128]{2,1,0:T(8,128)(2,1)S(1)} %all-to-all-done.own_ref.refs_0_), channel_id=1, source_target_pairs={{0,6},{2,4},{4,2},{6,0},{1,7},{3,5},{5,3},{7,1},{8,14},{10,12},{12... | collective-permute-start | bytes 786440 | tf_op jit(solution)/shard_map/ppermute | solution.py:42
  66.0 1.6 %collective-permute-start.6 = (bf16[32,32,128]{2,1,0:T(8,128)(2,1)S(1)}, bf16[32,32,128]{2,1,0:T(8,128)(2,1)S(1)}, u32[]{:S(2)}, u32[]{:S(2)}) collective-permute-start(bf16[32,32,128]{2,1,0:T(8,128)(2,1)S(1)} %all-to-all-done.own_ref.refs_0_), channel_id=1, source_target_pairs={{0,4},{2,6},{4,0},{6,2},{1,5},{3,7},{5,1},{7,3},{8,12},{10,14},{12... | collective-permute-start | bytes 786440 | tf_op jit(solution)/shard_map/ppermute | solution.py:42
  67.6 1.3 %shard_map.98 = bf16[32,4,8,128]{3,2,1,0:T(8,128)(2,1)} custom-call(s32[3]{0:T(128)S(1)} %pad_add_fusion.s_ref._, f32[32,128]{1,0:T(8,128)S(1)} %get-tuple-element.18.held_ref, f32[32,128]{1,0:T(8,128)S(1)} %get-tuple-element.17.allowed_ref, f32[2,8,128]{2,1,0:T(8,128)S(1)} %get-tuple-element.19.mine_ref, f32[2,8,128]{2,1,0:T(8,128)S(1)} %collective-permute-done.4.theirs_ref), custom_call_target="tpu_custom_call" | custom-call | bytes 311296 | tf_op jit(solution)/shard_map/pallas_call | solution.py:27
  68.9 8.8 %all-to-all-start.2 = ((bf16[128,8,128]{2,1,0:T(8,128)(2,1)}), bf16[128,8,128]{2,1,0:T(8,128)(2,1)S(1)}, u32[]{:S(2)}, u32[]{:S(2)}) async-start(bf16[128,8,128]{2,1,0:T(8,128)(2,1)} %bitcast.12), calls=%async_computation.2 | async-start | bytes 524288 | tf_op jit(solution)/shard_map/all_to_all | solution.py:323
  77.7 1.3 %collective-permute-start.10 = (bf16[32,32,128]{2,1,0:T(8,128)(2,1)S(1)}, bf16[32,32,128]{2,1,0:T(8,128)(2,1)S(1)}, u32[]{:S(2)}, u32[]{:S(2)}) collective-permute-start(bf16[32,32,128]{2,1,0:T(8,128)(2,1)S(1)} %collective-permute-done.7.refs_3_), channel_id=1, source_target_pairs={{0,1},{1,0},{2,3},{3,2},{4,5},{5,4},{6,7},{7,6},{8,9},{9,8},{10,11... | collective-permute-start | bytes 786440 | tf_op jit(solution)/shard_map/ppermute | solution.py:42
  82.7 7.0 %all-to-all-done.2 = bf16[128,8,128]{2,1,0:T(8,128)(2,1)S(1)} async-done(((bf16[128,8,128]{2,1,0:T(8,128)(2,1)}), bf16[128,8,128]{2,1,0:T(8,128)(2,1)S(1)}, u32[]{:S(2)}, u32[]{:S(2)}) %all-to-all-start.2) | async-done | bytes 262176 | tf_op jit(solution)/shard_map/all_to_all | solution.py:323
  91.4 1.6 %shard_map.100 = (f32[2,128,512]{2,1,0:T(8,128)S(1)}, f32[64,512]{1,0:T(8,128)S(1)}, bf16[64,512]{1,0:T(8,128)(2,1)S(1)}) custom-call(s32[3]{0:T(128)S(1)} %pad_add_fusion.s_ref._, bf16[32,4,8,128]{3,2,1,0:T(8,128)(2,1)S(1)} %bitcast.20, bf16[2,1,128,512]{3,2,1,0:T(8,128)(2,1)S(1)} %slice.3.slices_ref, f32[2,128,128]{2,1,0:T(8,128)S(1)} %shard_map.99.turn_ref, ...), custom_call_target="tpu_custom_call" | custom-call | flops 268435456 | bytes 3506176 | tf_op jit(solution)/shard_map/pallas_call | solution.py:27
  93.0 3.6 %collective-permute-start.11 = (bf16[64,512]{1,0:T(8,128)(2,1)S(1)}, bf16[64,512]{1,0:T(8,128)(2,1)S(1)}, u32[]{:S(2)}, u32[]{:S(2)}) collective-permute-start(bf16[64,512]{1,0:T(8,128)(2,1)S(1)} %get-tuple-element.24), channel_id=1, source_target_pairs={{0,1},{1,0},{2,3},{3,2},{4,5},{5,4},{6,7},{7,6},{8,9},{9,8},{10,11... | collective-permute-start | bytes 196616 | tf_op jit(solution)/shard_map/ppermute | solution.py:42
  97.8 1.5 %collective-permute-start.13 = (bf16[64,512]{1,0:T(8,128)(2,1)S(1)}, bf16[64,512]{1,0:T(8,128)(2,1)S(1)}, u32[]{:S(2)}, u32[]{:S(2)}) collective-permute-start(bf16[64,512]{1,0:T(8,128)(2,1)S(1)} %add_convert_fusion), channel_id=1, source_target_pairs={{0,4},{2,6},{4,0},{6,2},{1,5},{3,7},{5,1},{7,3},{8,12},{10,14},{12... | collective-permute-start | bytes 196616 | tf_op jit(solution)/shard_map/ppermute | solution.py:42
  99.2 2.2 %collective-permute-start.14 = (bf16[64,512]{1,0:T(8,128)(2,1)S(1)}, bf16[64,512]{1,0:T(8,128)(2,1)S(1)}, u32[]{:S(2)}, u32[]{:S(2)}) collective-permute-start(bf16[64,512]{1,0:T(8,128)(2,1)S(1)} %add_convert_fusion), channel_id=1, source_target_pairs={{0,6},{2,4},{4,2},{6,0},{1,7},{3,5},{5,3},{7,1},{8,14},{10,12},{12... | collective-permute-start | bytes 196616 | tf_op jit(solution)/shard_map/ppermute | solution.py:42
  102.4 1.8 %collective-permute-done.14 = bf16[64,512]{1,0:T(8,128)(2,1)S(1)} collective-permute-done((bf16[64,512]{1,0:T(8,128)(2,1)S(1)}, bf16[64,512]{1,0:T(8,128)(2,1)S(1)}, u32[]{:S(2)}, u32[]{:S(2)}) %collective-permute-start.14) | collective-permute-done | bytes 65568 | tf_op jit(solution)/shard_map/ppermute | solution.py:42
  104.2 1.6 %collective-permute-start.15 = (f32[64,512]{1,0:T(8,128)S(1)}, f32[64,512]{1,0:T(8,128)S(1)}, u32[]{:S(2)}, u32[]{:S(2)}) collective-permute-start(f32[64,512]{1,0:T(8,128)S(1)} %convert_add_fusion.mine_ref), channel_id=1, source_target_pairs={{0,1},{1,0},{2,3},{3,2},{4,5},{5,4},{6,7},{7,6},{8,9},{9,8},{10,11... | collective-permute-start | bytes 393224 | tf_op jit(solution)/shard_map/ppermute | solution.py:42
  105.8 1.5 %shard_map.101 = (f32[1016,128]{1,0:T(8,128)}, f32[32,128]{1,0:T(8,128)}) custom-call(s32[3]{0:T(128)S(1)} %pad_add_fusion.s_ref._, f32[2,128,512]{2,1,0:T(8,128)S(1)} %get-tuple-element.20.sums_ref, bf16[32,32,128]{2,1,0:T(8,128)(2,1)S(1)} %bitcast.21), custom_call_target="tpu_custom_call" | custom-call | bytes 1323008 | tf_op jit(solution)/shard_map/pallas_call | solution.py:27
  107.3 1.3 %shard_map.102 = f32[64,2,508]{2,1,0:T(2,128)} custom-call(s32[3]{0:T(128)S(1)} %pad_add_fusion.s_ref._, f32[64,512]{1,0:T(8,128)S(1)} %convert_add_fusion.mine_ref, f32[64,512]{1,0:T(8,128)S(1)} %collective-permute-done.15.theirs_ref), custom_call_target="tpu_custom_call" | custom-call | bytes 522240 | tf_op jit(solution)/shard_map/pallas_call | solution.py:27
  (50 shorter events, 11.5 us)
Async XLA Ops:
  0.6 15.9 %copy-start.7 = (bf16[128,64]{0,1:T(8,128)(2,1)S(1)}, bf16[128,64]{0,1:T(8,128)(2,1)}, u32[]{:S(2)}) copy-start(bf16[128,64]{0,1:T(8,128)(2,1)} %param.12) | copy-start | bytes 49156
  0.6 29.2 %copy-start.4 = (f32[128]{0:T(128)S(1)}, f32[128]{0:T(128)}, u32[]{:S(2)}) copy-start(f32[128]{0:T(128)} %param.13) | copy-start | bytes 1540
  0.7 33.2 %copy-start.6 = (bf16[64,2,508]{2,1,0:T(2,128)(2,1)S(1)}, bf16[64,2,508]{2,1,0:T(2,128)(2,1)}, u32[]{:S(2)}) copy-start(bf16[64,2,508]{2,1,0:T(2,128)(2,1)} %param.11) | copy-start | bytes 390148
  0.7 36.5 %copy-start.3 = (s32[1,512]{1,0:T(1,128)S(1)}, s32[1,512]{1,0:T(1,128)}, u32[]{:S(2)}) copy-start(s32[1,512]{1,0:T(1,128)} %param.10) | copy-start | bytes 6148
  0.7 36.5 %copy-start.5 = (f32[32]{0:T(128)S(1)}, f32[32]{0:T(128)}, u32[]{:S(2)}) copy-start(f32[32]{0:T(128)} %temp_ref.1) | copy-start | bytes 388
  4.4 21.7 %all-to-all-start = ((bf16[32,32,128]{2,1,0:T(8,128)(2,1)}), bf16[32,32,128]{2,1,0:T(8,128)(2,1)S(1)}, u32[]{:S(2)}, u32[]{:S(2)}) async-start(bf16[32,32,128]{2,1,0:T(8,128)(2,1)} %bitcast.25), calls=%async_computation | async-start | bytes 524288 | tf_op jit(solution)/shard_map/all_to_all | solution.py:272
  26.1 13.5 %collective-permute-start = (bf16[32,32,128]{2,1,0:T(8,128)(2,1)S(1)}, bf16[32,32,128]{2,1,0:T(8,128)(2,1)S(1)}, u32[]{:S(2)}, u32[]{:S(2)}) collective-permute-start(bf16[32,32,128]{2,1,0:T(8,128)(2,1)S(1)} %all-to-all-done.own_ref.refs_0_), channel_id=1, source_target_pairs={{0,1},{1,0},{2,3},{3,2},{4,5},{5,4},{6,7},{7,6},{8,9},{9,8},{10,11... | collective-permute-start | bytes 786440 | tf_op jit(solution)/shard_map/ppermute | solution.py:42
  29.9 4.9 %collective-permute-start.3 = (f32[128,128]{1,0:T(8,128)S(1)}, f32[128,128]{1,0:T(8,128)S(1)}, u32[]{:S(2)}, u32[]{:S(2)}) collective-permute-start(f32[128,128]{1,0:T(8,128)S(1)} %get-tuple-element.26), channel_id=1, source_target_pairs={{0,6},{2,4},{4,2},{6,0},{1,7},{3,5},{5,3},{7,1},{8,14},{10,12},{12... | collective-permute-start | bytes 196616 | tf_op jit(solution)/shard_map/ppermute | solution.py:42
  32.5 3.1 %collective-permute-start.1 = (f32[128,128]{1,0:T(8,128)S(1)}, f32[128,128]{1,0:T(8,128)S(1)}, u32[]{:S(2)}, u32[]{:S(2)}) collective-permute-start(f32[128,128]{1,0:T(8,128)S(1)} %get-tuple-element.26), channel_id=1, source_target_pairs={{0,2},{2,0},{4,6},{6,4},{1,3},{3,1},{5,7},{7,5},{8,10},{10,8},{12,... | collective-permute-start | bytes 196616 | tf_op jit(solution)/shard_map/ppermute | solution.py:42
  32.5 4.6 %collective-permute-start.2 = (f32[128,128]{1,0:T(8,128)S(1)}, f32[128,128]{1,0:T(8,128)S(1)}, u32[]{:S(2)}, u32[]{:S(2)}) collective-permute-start(f32[128,128]{1,0:T(8,128)S(1)} %get-tuple-element.26), channel_id=1, source_target_pairs={{0,4},{2,6},{4,0},{6,2},{1,5},{3,7},{5,1},{7,3},{8,12},{10,14},{12... | collective-permute-start | bytes 196616 | tf_op jit(solution)/shard_map/ppermute | solution.py:42
  58.6 9.0 %collective-permute-start.4 = (f32[2,8,128]{2,1,0:T(8,128)S(1)}, f32[2,8,128]{2,1,0:T(8,128)S(1)}, u32[]{:S(2)}, u32[]{:S(2)}) collective-permute-start(f32[2,8,128]{2,1,0:T(8,128)S(1)} %get-tuple-element.19.mine_ref), channel_id=1, source_target_pairs={{0,1},{1,0},{2,3},{3,2},{4,5},{5,4},{6,7},{7,6},{8,9},{9,8},{10,11... | collective-permute-start | bytes 24584 | tf_op jit(solution)/shard_map/ppermute | solution.py:42
  63.7 13.9 %collective-permute-start.7 = (bf16[32,32,128]{2,1,0:T(8,128)(2,1)S(1)}, bf16[32,32,128]{2,1,0:T(8,128)(2,1)S(1)}, u32[]{:S(2)}, u32[]{:S(2)}) collective-permute-start(bf16[32,32,128]{2,1,0:T(8,128)(2,1)S(1)} %all-to-all-done.own_ref.refs_0_), channel_id=1, source_target_pairs={{0,6},{2,4},{4,2},{6,0},{1,7},{3,5},{5,3},{7,1},{8,14},{10,12},{12... | collective-permute-start | bytes 786440 | tf_op jit(solution)/shard_map/ppermute | solution.py:42
  66.0 13.0 %collective-permute-start.5 = (bf16[32,32,128]{2,1,0:T(8,128)(2,1)S(1)}, bf16[32,32,128]{2,1,0:T(8,128)(2,1)S(1)}, u32[]{:S(2)}, u32[]{:S(2)}) collective-permute-start(bf16[32,32,128]{2,1,0:T(8,128)(2,1)S(1)} %all-to-all-done.own_ref.refs_0_), channel_id=1, source_target_pairs={{0,2},{2,0},{4,6},{6,4},{1,3},{3,1},{5,7},{7,5},{8,10},{10,8},{12,... | collective-permute-start | bytes 786440 | tf_op jit(solution)/shard_map/ppermute | solution.py:42
  66.0 13.3 %collective-permute-start.6 = (bf16[32,32,128]{2,1,0:T(8,128)(2,1)S(1)}, bf16[32,32,128]{2,1,0:T(8,128)(2,1)S(1)}, u32[]{:S(2)}, u32[]{:S(2)}) collective-permute-start(bf16[32,32,128]{2,1,0:T(8,128)(2,1)S(1)} %all-to-all-done.own_ref.refs_0_), channel_id=1, source_target_pairs={{0,4},{2,6},{4,0},{6,2},{1,5},{3,7},{5,1},{7,3},{8,12},{10,14},{12... | collective-permute-start | bytes 786440 | tf_op jit(solution)/shard_map/ppermute | solution.py:42
  68.9 20.8 %all-to-all-start.2 = ((bf16[128,8,128]{2,1,0:T(8,128)(2,1)}), bf16[128,8,128]{2,1,0:T(8,128)(2,1)S(1)}, u32[]{:S(2)}, u32[]{:S(2)}) async-start(bf16[128,8,128]{2,1,0:T(8,128)(2,1)} %bitcast.12), calls=%async_computation.2 | async-start | bytes 524288 | tf_op jit(solution)/shard_map/all_to_all | solution.py:323
  77.7 4.3 %collective-permute-start.10 = (bf16[32,32,128]{2,1,0:T(8,128)(2,1)S(1)}, bf16[32,32,128]{2,1,0:T(8,128)(2,1)S(1)}, u32[]{:S(2)}, u32[]{:S(2)}) collective-permute-start(bf16[32,32,128]{2,1,0:T(8,128)(2,1)S(1)} %collective-permute-done.7.refs_3_), channel_id=1, source_target_pairs={{0,1},{1,0},{2,3},{3,2},{4,5},{5,4},{6,7},{7,6},{8,9},{9,8},{10,11... | collective-permute-start | bytes 786440 | tf_op jit(solution)/shard_map/ppermute | solution.py:42
  79.0 3.0 %collective-permute-start.8 = (bf16[32,32,128]{2,1,0:T(8,128)(2,1)S(1)}, bf16[32,32,128]{2,1,0:T(8,128)(2,1)S(1)}, u32[]{:S(2)}, u32[]{:S(2)}) collective-permute-start(bf16[32,32,128]{2,1,0:T(8,128)(2,1)S(1)} %collective-permute-done.5.refs_1_), channel_id=1, source_target_pairs={{0,1},{1,0},{2,3},{3,2},{4,5},{5,4},{6,7},{7,6},{8,9},{9,8},{10,11... | collective-permute-start | bytes 786440 | tf_op jit(solution)/shard_map/ppermute | solution.py:42
  79.3 2.7 %collective-permute-start.9 = (bf16[32,32,128]{2,1,0:T(8,128)(2,1)S(1)}, bf16[32,32,128]{2,1,0:T(8,128)(2,1)S(1)}, u32[]{:S(2)}, u32[]{:S(2)}) collective-permute-start(bf16[32,32,128]{2,1,0:T(8,128)(2,1)S(1)} %collective-permute-done.6.refs_2_), channel_id=1, source_target_pairs={{0,1},{1,0},{2,3},{3,2},{4,5},{5,4},{6,7},{7,6},{8,9},{9,8},{10,11... | collective-permute-start | bytes 786440 | tf_op jit(solution)/shard_map/ppermute | solution.py:42
  89.7 1.0 copy-start.1
  93.0 4.5 %collective-permute-start.11 = (bf16[64,512]{1,0:T(8,128)(2,1)S(1)}, bf16[64,512]{1,0:T(8,128)(2,1)S(1)}, u32[]{:S(2)}, u32[]{:S(2)}) collective-permute-start(bf16[64,512]{1,0:T(8,128)(2,1)S(1)} %get-tuple-element.24), channel_id=1, source_target_pairs={{0,1},{1,0},{2,3},{3,2},{4,5},{5,4},{6,7},{7,6},{8,9},{9,8},{10,11... | collective-permute-start | bytes 196616 | tf_op jit(solution)/shard_map/ppermute | solution.py:42
  97.5 3.9 %collective-permute-start.12 = (bf16[64,512]{1,0:T(8,128)(2,1)S(1)}, bf16[64,512]{1,0:T(8,128)(2,1)S(1)}, u32[]{:S(2)}, u32[]{:S(2)}) collective-permute-start(bf16[64,512]{1,0:T(8,128)(2,1)S(1)} %add_convert_fusion), channel_id=1, source_target_pairs={{0,2},{2,0},{4,6},{6,4},{1,3},{3,1},{5,7},{7,5},{8,10},{10,8},{12,... | collective-permute-start | bytes 196616 | tf_op jit(solution)/shard_map/ppermute | solution.py:42
  97.8 4.7 %collective-permute-start.13 = (bf16[64,512]{1,0:T(8,128)(2,1)S(1)}, bf16[64,512]{1,0:T(8,128)(2,1)S(1)}, u32[]{:S(2)}, u32[]{:S(2)}) collective-permute-start(bf16[64,512]{1,0:T(8,128)(2,1)S(1)} %add_convert_fusion), channel_id=1, source_target_pairs={{0,4},{2,6},{4,0},{6,2},{1,5},{3,7},{5,1},{7,3},{8,12},{10,14},{12... | collective-permute-start | bytes 196616 | tf_op jit(solution)/shard_map/ppermute | solution.py:42
  99.2 4.9 %collective-permute-start.14 = (bf16[64,512]{1,0:T(8,128)(2,1)S(1)}, bf16[64,512]{1,0:T(8,128)(2,1)S(1)}, u32[]{:S(2)}, u32[]{:S(2)}) collective-permute-start(bf16[64,512]{1,0:T(8,128)(2,1)S(1)} %add_convert_fusion), channel_id=1, source_target_pairs={{0,6},{2,4},{4,2},{6,0},{1,7},{3,5},{5,3},{7,1},{8,14},{10,12},{12... | collective-permute-start | bytes 196616 | tf_op jit(solution)/shard_map/ppermute | solution.py:42
  104.2 3.1 %collective-permute-start.15 = (f32[64,512]{1,0:T(8,128)S(1)}, f32[64,512]{1,0:T(8,128)S(1)}, u32[]{:S(2)}, u32[]{:S(2)}) collective-permute-start(f32[64,512]{1,0:T(8,128)S(1)} %convert_add_fusion.mine_ref), channel_id=1, source_target_pairs={{0,1},{1,0},{2,3},{3,2},{4,5},{5,4},{6,7},{7,6},{8,9},{9,8},{10,11... | collective-permute-start | bytes 393224 | tf_op jit(solution)/shard_map/ppermute | solution.py:42
  (2 other events, 1.5 us)

commit v2 on v1

--- a/solution.py
+++ b/solution.py
@@ -108,10 +108,29 @@
     )(shifts, images)
 
 
-def slices_kernel(width):
+def slices_of(packed, volume_ref, order, slices_ref):
+    degrees = volume_ref.shape[1]
+    block = packed.astype(jnp.float32).T
+    azimuth = sum(block[:, degrees + k : degrees + k + 1] for k in range(3))
+    angles = jnp.broadcast_to(azimuth, (LANES, LANES)) * order
+    cosine, sine = jnp.cos(angles), jnp.sin(angles)
+    tilts = block[:, :degrees].astype(jnp.bfloat16)
+    power = jnp.zeros((LANES, LANES), jnp.float32)
+    for t in range(volume_ref.shape[2] // LANES):
+        at = slice(t * LANES, (t + 1) * LANES)
+        re = jnp.dot(tilts, volume_ref[0, :, at], preferred_element_type=jnp.float32)
+        im = jnp.dot(tilts, volume_ref[1, :, at], preferred_element_type=jnp.float32)
+        first = (re * cosine - im * sine).astype(jnp.bfloat16)
+        second = (re * sine + im * cosine).astype(jnp.bfloat16)
+        slices_ref[0, :, at] = first
+        slices_ref[1, :, at] = second
+        power += jnp.square(first.astype(jnp.float32)) + jnp.square(second.astype(jnp.float32))
+    return 0.5 * jnp.sum(power.T, axis=0, keepdims=True)
+
+
+def own_slices_kernel(width, across_x):
     def kernel(s_ref, temp_ref, listed_ref, packed_ref, volume_ref, slices_ref, half_ref, temps_ref, allowed_ref):
         c, x = s_ref[0], s_ref[1]
-        degrees = volume_ref.shape[1]
         row = lax.broadcasted_iota(jnp.int32, (ROWS, LANES), 0)
         temps = jnp.zeros((ROWS, LANES), jnp.float32)
         for n in range(ROWS):
@@ -121,8 +140,7 @@
             for k in range(listed_ref.shape[0])
         ]
         lane = lax.broadcasted_iota(jnp.int32, (1, LANES), 1)
-        order = orders(s_ref[2] * width)
-        for d in range(packed_ref.shape[0]):
+        for d in range(across_x):
             ids = (((x ^ d) * 2 + c) * LANES + lane).astype(jnp.float32)
             found = jnp.zeros((LANES, LANES), jnp.float32)
             for one in listed:
@@ -131,21 +149,17 @@
                 jnp.max(found, axis=0, keepdims=True), (ROWS, LANES)
             )
             temps_ref[d * ROWS : (d + 1) * ROWS, :] = temps
-            block = packed_ref[d].T
-            angles = jnp.broadcast_to(block[:, degrees : degrees + 1], block.shape) * order
-            cosine, sine = jnp.cos(angles), jnp.sin(angles)
-            tilts = block[:, :degrees].astype(jnp.bfloat16)
-            power = jnp.zeros_like(block)
-            for t in range(volume_ref.shape[2] // LANES):
-                at = slice(t * LANES, (t + 1) * LANES)
-                re = jnp.dot(tilts, volume_ref[0, :, at], preferred_element_type=jnp.float32)
-                im = jnp.dot(tilts, volume_ref[1, :, at], preferred_element_type=jnp.float32)
-                first = (re * cosine - im * sine).astype(jnp.bfloat16)
-                second = (re * sine + im * cosine).astype(jnp.bfloat16)
-                slices_ref[0, d, :, at] = first
-                slices_ref[1, d, :, at] = second
-                power += jnp.square(first.astype(jnp.float32)) + jnp.square(second.astype(jnp.float32))
-            half_ref[d : d + 1, :] = 0.5 * jnp.sum(power.T, axis=0, keepdims=True)
+        half_ref[...] = slices_of(packed_ref[...], volume_ref, orders(s_ref[2] * width), slices_ref)
+
+    return kernel
+
+
+def slices_kernel(width):
+    def kernel(s_ref, volume_ref, *refs):
+        *blocks, slices_ref, half_ref = refs
+        order = orders(s_ref[2] * width)
+        for d, packed_ref in enumerate(blocks):
+            half_ref[d : d + 1, :] = slices_of(packed_ref[...], volume_ref, order, slices_ref.at[d])
 
     return kernel
 
@@ -165,16 +179,18 @@
     return jnp.concatenate(pieces, axis=1)
 
 
-def inner_kernel(s_ref, own_ref, other_ref, slices_ref, half_ref, out_ref):
+def inner_kernel(s_ref, own_ref, other_ref, near_ref, near_half_ref, far_ref, far_half_ref, out_ref):
     c = s_ref[0]
     groups = own_ref.shape[0]
     rows = groups * ROWS
     own, other = wide(own_ref, rows), wide(other_ref, rows)
     dims = (((1,), (1,)), ((), ()))
-    for d in range(slices_ref.shape[1]):
-        acc = lax.dot_general(own, slices_ref[c, d], dims, preferred_element_type=jnp.float32)
-        acc += lax.dot_general(other, slices_ref[1 - c, d], dims, preferred_element_type=jnp.float32)
-        acc = acc - half_ref[d : d + 1, :]
+    blocks = [(near_ref, near_half_ref[...])]
+    blocks += [(far_ref.at[d], far_half_ref[d : d + 1, :]) for d in range(far_ref.shape[0])]
+    for d, (slices, half) in enumerate(blocks):
+        acc = lax.dot_general(own, slices[c], dims, preferred_element_type=jnp.float32)
+        acc += lax.dot_general(other, slices[1 - c], dims, preferred_element_type=jnp.float32)
+        acc = acc - half
         out_ref[:, d * ROWS : (d + 1) * ROWS, :] = acc.reshape(groups, ROWS, LANES)
 
 
@@ -230,8 +246,8 @@
     cosine, sine = turn_ref[0], turn_ref[1]
     for t in range(tiles):
         at = slice(t * LANES, (t + 1) * LANES)
-        first = sums_ref[0, :, at] - mass * slices_ref[0, 0, :, at].astype(jnp.float32)
-        second = sums_ref[1, :, at] - mass * slices_ref[1, 0, :, at].astype(jnp.float32)
+        first = sums_ref[0, :, at] - mass * slices_ref[0, :, at].astype(jnp.float32)
+        second = sums_ref[1, :, at] - mass * slices_ref[1, :, at].astype(jnp.float32)
         grads = []
         for back in (first * cosine + second * sine, second * cosine - first * sine):
             high = back.astype(jnp.bfloat16)
@@ -272,27 +288,35 @@
     mine = lax.all_to_all(cut.reshape(groups, tiles * ROWS, LANES), "img", 0, 0, tiled=True)
     other = across(mine, "c", 1)
 
-    packed = jnp.concatenate(
-        [tilts.T.astype(jnp.float32), azimuth[None, :], jnp.zeros((LANES - degrees - 1, orients), jnp.float32)], axis=0
-    )
-    gathered = [packed]
+    high = lax.reduce_precision(azimuth, 8, 7)
+    middle = lax.reduce_precision(azimuth - high, 8, 7)
+    terms = jnp.stack([high, middle, azimuth - high - middle]).astype(jnp.bfloat16)
+    packed = jnp.concatenate([tilts.T, jnp.pad(terms, ((0, 2 * ROWS - 3), (0, 0)))], axis=0)
+    gathered = []
     for d in range(1, across_x):
         gathered.append(across(packed, "x", d))
-    gathered = jnp.stack(gathered)
     pad = jnp.pad(jnp.swapaxes(volume, 0, 1), ((0, 0), (0, 0), (0, padded - width)))
-    slices, half, temps, allowed = call(
-        slices_kernel(width),
+    near, near_half, temps, allowed = call(
+        own_slices_kernel(width, across_x),
         (
-            shape((2, across_x, orients, padded), jnp.bfloat16),
-            shape((across_x, LANES)),
+            shape((2, orients, padded), jnp.bfloat16),
+            shape((1, LANES)),
             shape((across_x * ROWS, LANES)),
             shape((across_x * ROWS, LANES)),
         ),
         (scalars, inv_temp),
         candidates.reshape(-1, LANES),
-        gathered,
+        packed,
         pad,
-        flops=4 * across_x * orients * degrees * padded,
+        flops=4 * orients * degrees * padded,
+    )
+    far, far_half = call(
+        slices_kernel(width),
+        (shape((across_x - 1, 2, orients, padded), jnp.bfloat16), shape((across_x - 1, LANES))),
+        scalars,
+        pad,
+        *gathered,
+        flops=4 * (across_x - 1) * orients * degrees * padded,
     )
 
     partial = call(
@@ -301,8 +325,10 @@
         scalars,
         mine,
         other,
-        slices,
-        half,
+        near,
+        near_half,
+        far,
+        far_half,
         flops=4 * groups * ROWS * padded * across_x * LANES,
     )
     partial = lax.all_to_all(partial, "img", 0, 0, tiled=True)
@@ -334,7 +360,7 @@
         (shape((2, orients, padded)), shape((degrees, padded)), shape((degrees, padded), jnp.bfloat16)),
         scalars,
         posts,
-        slices[:, :1],
+        near,
         turns,
         turned,
         *mine_all,

time: 109 us -> 105 us (0.963)
  local copies, waits for them, and re-layouts: 2.55 us -> 0.05 us
  starting transfers between devices: 49.4 us -> 48 us
    unnamed x17 -> x11, local copies, waits for them, and re-layouts: 2.44 us -> 0.04 us
    all_to_all x1, starting transfers between devices: 8.76 us -> 7.07 us  [shards(): posts = lax.all_to_all(copies, ('img', 'x'), 0, 0, tiled=True)]
    pallas_call x8 -> x9, Pallas kernels: 11 us -> 11.9 us  [call(): pl.pallas_call(kernel, out_shape=out_shape, in_specs=specs, out_specs=out...]
  transfers between devices with their start and end apart: 18 -> 18, of which waited for: 8 -> 9; matrix products, arithmetic and copies ran while one was open for 1% -> 0% of each run, Pallas kernels for 6% -> 7%
where the time goes in v2:
time: 105 us
  starting transfers between devices  48 us (46%)
  waiting for transfers between devices  23.5 us (22%)
  blocking collectives  17 us (16%)
  Pallas kernels  15.6 us (15%)
    ppermute x16, starting transfers between devices, across(): lax.ppermute(x, axis, [(s, s ^ turn) for s in range(lax.axis_size(axis))])  28.9 us
    all_to_all x1, blocking collectives, shards(): partial = lax.all_to_all(partial, 'img', 0, 0, tiled=True)  17 us
    all_to_all x1, starting transfers between devices, shards(): lax.all_to_all(cut.reshape(groups, tiles * ROWS, LANES), 'img', 0, 0, til...  12 us
    pallas_call x9, Pallas kernels, call(): pl.pallas_call(kernel, out_shape=out_shape, in_specs=specs, out_specs=out...  11.9 us
    all_to_all x1, waiting for transfers between devices, shards(): lax.all_to_all(cut.reshape(groups, tiles * ROWS, LANES), 'img', 0, 0, til...  9.66 us
    ppermute x16, waiting for transfers between devices, across(): lax.ppermute(x, axis, [(s, s ^ turn) for s in range(lax.axis_size(axis))])  7.8 us
    all_to_all x1, starting transfers between devices, shards(): posts = lax.all_to_all(copies, ('img', 'x'), 0, 0, tiled=True)  7.07 us
    all_to_all x1, waiting for transfers between devices, shards(): posts = lax.all_to_all(copies, ('img', 'x'), 0, 0, tiled=True)  6.01 us
  transfers between devices with their start and end apart: 18, of which 9 were waited for; matrix products, arithmetic and copies ran while one was open for 0% of the time, Pallas kernels for 7%

profile of v2, /device:TPU:1, one launch (start us, length us, event | category | flops | bytes accessed | tf_op | source)
XLA Modules:
  0.0 105.1 jit_solution(11509130012139638922)
XLA Ops:
  0.7 3.7 %shard_map.94 = bf16[32,4,8,128]{3,2,1,0:T(8,128)(2,1)} custom-call(s32[32]{0:T(128)} %shifts_ref.1, bf16[32,2,16256]{2,1,0:T(2,128)(2,1)} %images_ref.1), custom_call_target="tpu_custom_call" | custom-call | tf_op jit(solution)/shard_map/pallas_call | solution.py:101
  4.4 12.0 %all-to-all-start = ((bf16[32,32,128]{2,1,0:T(8,128)(2,1)}), bf16[32,32,128]{2,1,0:T(8,128)(2,1)S(1)}, u32[]{:S(2)}, u32[]{:S(2)}) async-start(bf16[32,32,128]{2,1,0:T(8,128)(2,1)} %bitcast.24), calls=%async_computation | async-start | bytes 524288 | tf_op jit(solution)/shard_map/all_to_all | solution.py:288
  16.5 9.7 %all-to-all-done.own_ref.refs_0_ = bf16[32,32,128]{2,1,0:T(8,128)(2,1)S(1)} async-done(((bf16[32,32,128]{2,1,0:T(8,128)(2,1)}), bf16[32,32,128]{2,1,0:T(8,128)(2,1)S(1)}, u32[]{:S(2)}, u32[]{:S(2)}) %all-to-all-start) | async-done | bytes 262176 | tf_op jit(solution)/shard_map/all_to_all | solution.py:288
  26.1 3.7 %collective-permute-start = (bf16[32,32,128]{2,1,0:T(8,128)(2,1)S(1)}, bf16[32,32,128]{2,1,0:T(8,128)(2,1)S(1)}, u32[]{:S(2)}, u32[]{:S(2)}) collective-permute-start(bf16[32,32,128]{2,1,0:T(8,128)(2,1)S(1)} %all-to-all-done.own_ref.refs_0_), channel_id=1, source_target_pairs={{0,1},{1,0},{2,3},{3,2},{4,5},{5,4},{6,7},{7,6},{8,9},{9,8},{10,11... | collective-permute-start | bytes 786440 | tf_op jit(solution)/shard_map/ppermute | solution.py:42
  29.9 1.3 %collective-permute-start.1 = (bf16[80,128]{1,0:T(8,128)(2,1)S(1)}, bf16[80,128]{1,0:T(8,128)(2,1)S(1)}, u32[]{:S(2)}, u32[]{:S(2)}) collective-permute-start(bf16[80,128]{1,0:T(8,128)(2,1)S(1)} %pad_maximum_fusion.1.packed_ref), channel_id=1, source_target_pairs={{0,2},{2,0},{4,6},{6,4},{1,3},{3,1},{5,7},{7,5},{8,10},{10,8},{12,... | collective-permute-start | bytes 61448 | tf_op jit(solution)/shard_map/ppermute | solution.py:42
  31.2 2.5 %collective-permute-start.2 = (bf16[80,128]{1,0:T(8,128)(2,1)S(1)}, bf16[80,128]{1,0:T(8,128)(2,1)S(1)}, u32[]{:S(2)}, u32[]{:S(2)}) collective-permute-start(bf16[80,128]{1,0:T(8,128)(2,1)S(1)} %pad_maximum_fusion.1.packed_ref), channel_id=1, source_target_pairs={{0,4},{2,6},{4,0},{6,2},{1,5},{3,7},{5,1},{7,3},{8,12},{10,14},{12... | collective-permute-start | bytes 61448 | tf_op jit(solution)/shard_map/ppermute | solution.py:42
  35.5 2.0 %collective-permute-done.3.refs_2_ = bf16[80,128]{1,0:T(8,128)(2,1)S(1)} collective-permute-done((bf16[80,128]{1,0:T(8,128)(2,1)S(1)}, bf16[80,128]{1,0:T(8,128)(2,1)S(1)}, u32[]{:S(2)}, u32[]{:S(2)}) %collective-permute-start.3) | collective-permute-done | bytes 20512 | tf_op jit(solution)/shard_map/ppermute | solution.py:42
  37.5 2.0 %shard_map.96 = (bf16[3,2,128,512]{3,2,1,0:T(8,128)(2,1)S(1)}, f32[3,128]{1,0:T(4,128)S(1)}) custom-call(s32[3]{0:T(128)S(1)} %pad_add_fusion.s_ref._, bf16[2,64,512]{2,1,0:T(8,128)(2,1)S(1)} %pad.9.volume_ref, bf16[80,128]{1,0:T(8,128)(2,1)S(1)} %collective-permute-done.1.refs_0_, bf16[80,128]{1,0:T(8,128)(2,1)S(1)} %collective-permute-done.2.refs_1_, ...), custom_call_target="tpu_custom_call" | custom-call | flops 50331648 | bytes 980480 | tf_op jit(solution)/shard_map/pallas_call | solution.py:27
  40.8 17.0 %all_to_all.15.parts_ref = f32[32,32,128]{2,1,0:T(8,128)S(1)} all-to-all(f32[32,32,128]{2,1,0:T(8,128)S(1)} %shard_map.97), channel_id=1, replica_groups=mesh['img'=32,'x'=4,'c'=2] {'img'}, dimensions={0} | all-to-all | bytes 1048576 | tf_op jit(solution)/shard_map/all_to_all | solution.py:334
  58.5 5.1 %collective-permute-start.4 = (f32[2,8,128]{2,1,0:T(8,128)S(1)}, f32[2,8,128]{2,1,0:T(8,128)S(1)}, u32[]{:S(2)}, u32[]{:S(2)}) collective-permute-start(f32[2,8,128]{2,1,0:T(8,128)S(1)} %get-tuple-element.23.mine_ref), channel_id=1, source_target_pairs={{0,1},{1,0},{2,3},{3,2},{4,5},{5,4},{6,7},{7,6},{8,9},{9,8},{10,11... | collective-permute-start | bytes 24584 | tf_op jit(solution)/shard_map/ppermute | solution.py:42
  64.1 3.3 %collective-permute-start.6 = (bf16[32,32,128]{2,1,0:T(8,128)(2,1)S(1)}, bf16[32,32,128]{2,1,0:T(8,128)(2,1)S(1)}, u32[]{:S(2)}, u32[]{:S(2)}) collective-permute-start(bf16[32,32,128]{2,1,0:T(8,128)(2,1)S(1)} %all-to-all-done.own_ref.refs_0_), channel_id=1, source_target_pairs={{0,4},{2,6},{4,0},{6,2},{1,5},{3,7},{5,1},{7,3},{8,12},{10,14},{12... | collective-permute-start | bytes 786440 | tf_op jit(solution)/shard_map/ppermute | solution.py:42
  68.7 7.1 %all-to-all-start.2 = ((bf16[128,8,128]{2,1,0:T(8,128)(2,1)}), bf16[128,8,128]{2,1,0:T(8,128)(2,1)S(1)}, u32[]{:S(2)}, u32[]{:S(2)}) async-start(bf16[128,8,128]{2,1,0:T(8,128)(2,1)} %bitcast.10), calls=%async_computation.2 | async-start | bytes 524288 | tf_op jit(solution)/shard_map/all_to_all | solution.py:349
  75.8 1.3 %collective-permute-start.10 = (bf16[32,32,128]{2,1,0:T(8,128)(2,1)S(1)}, bf16[32,32,128]{2,1,0:T(8,128)(2,1)S(1)}, u32[]{:S(2)}, u32[]{:S(2)}) collective-permute-start(bf16[32,32,128]{2,1,0:T(8,128)(2,1)S(1)} %collective-permute-done.7.refs_3_), channel_id=1, source_target_pairs={{0,1},{1,0},{2,3},{3,2},{4,5},{5,4},{6,7},{7,6},{8,9},{9,8},{10,11... | collective-permute-start | bytes 786440 | tf_op jit(solution)/shard_map/ppermute | solution.py:42
  77.4 1.6 %collective-permute-done.6.refs_2_ = bf16[32,32,128]{2,1,0:T(8,128)(2,1)S(1)} collective-permute-done((bf16[32,32,128]{2,1,0:T(8,128)(2,1)S(1)}, bf16[32,32,128]{2,1,0:T(8,128)(2,1)S(1)}, u32[]{:S(2)}, u32[]{:S(2)}) %collective-permute-start.6) | collective-permute-done | bytes 262176 | tf_op jit(solution)/shard_map/ppermute | solution.py:42
  79.1 1.6 %collective-permute-start.9 = (bf16[32,32,128]{2,1,0:T(8,128)(2,1)S(1)}, bf16[32,32,128]{2,1,0:T(8,128)(2,1)S(1)}, u32[]{:S(2)}, u32[]{:S(2)}) collective-permute-start(bf16[32,32,128]{2,1,0:T(8,128)(2,1)S(1)} %collective-permute-done.6.refs_2_), channel_id=1, source_target_pairs={{0,1},{1,0},{2,3},{3,2},{4,5},{5,4},{6,7},{7,6},{8,9},{9,8},{10,11... | collective-permute-start | bytes 786440 | tf_op jit(solution)/shard_map/ppermute | solution.py:42
  81.8 6.0 %all-to-all-done.2 = bf16[128,8,128]{2,1,0:T(8,128)(2,1)S(1)} async-done(((bf16[128,8,128]{2,1,0:T(8,128)(2,1)}), bf16[128,8,128]{2,1,0:T(8,128)(2,1)S(1)}, u32[]{:S(2)}, u32[]{:S(2)}) %all-to-all-start.2) | async-done | bytes 262176 | tf_op jit(solution)/shard_map/all_to_all | solution.py:349
  87.8 1.6 %shard_map.101 = (f32[2,128,512]{2,1,0:T(8,128)S(1)}, f32[64,512]{1,0:T(8,128)S(1)}, bf16[64,512]{1,0:T(8,128)(2,1)S(1)}) custom-call(s32[3]{0:T(128)S(1)} %pad_add_fusion.s_ref._, bf16[32,4,8,128]{3,2,1,0:T(8,128)(2,1)S(1)} %bitcast.20, bf16[2,128,512]{2,1,0:T(8,128)(2,1)S(1)} %get-tuple-element.16.near_ref.slices_ref, ...), custom_call_target="tpu_custom_call" | custom-call | flops 268435456 | bytes 3506176 | tf_op jit(solution)/shard_map/pallas_call | solution.py:27
  89.4 3.6 %collective-permute-start.11 = (bf16[64,512]{1,0:T(8,128)(2,1)S(1)}, bf16[64,512]{1,0:T(8,128)(2,1)S(1)}, u32[]{:S(2)}, u32[]{:S(2)}) collective-permute-start(bf16[64,512]{1,0:T(8,128)(2,1)S(1)} %get-tuple-element.28), channel_id=1, source_target_pairs={{0,1},{1,0},{2,3},{3,2},{4,5},{5,4},{6,7},{7,6},{8,9},{9,8},{10,11... | collective-permute-start | bytes 196616 | tf_op jit(solution)/shard_map/ppermute | solution.py:42
  94.2 1.5 %collective-permute-start.13 = (bf16[64,512]{1,0:T(8,128)(2,1)S(1)}, bf16[64,512]{1,0:T(8,128)(2,1)S(1)}, u32[]{:S(2)}, u32[]{:S(2)}) collective-permute-start(bf16[64,512]{1,0:T(8,128)(2,1)S(1)} %add_convert_fusion), channel_id=1, source_target_pairs={{0,4},{2,6},{4,0},{6,2},{1,5},{3,7},{5,1},{7,3},{8,12},{10,14},{12... | collective-permute-start | bytes 196616 | tf_op jit(solution)/shard_map/ppermute | solution.py:42
  95.7 2.2 %collective-permute-start.14 = (bf16[64,512]{1,0:T(8,128)(2,1)S(1)}, bf16[64,512]{1,0:T(8,128)(2,1)S(1)}, u32[]{:S(2)}, u32[]{:S(2)}) collective-permute-start(bf16[64,512]{1,0:T(8,128)(2,1)S(1)} %add_convert_fusion), channel_id=1, source_target_pairs={{0,6},{2,4},{4,2},{6,0},{1,7},{3,5},{5,3},{7,1},{8,14},{10,12},{12... | collective-permute-start | bytes 196616 | tf_op jit(solution)/shard_map/ppermute | solution.py:42
  98.9 1.7 %collective-permute-done.14 = bf16[64,512]{1,0:T(8,128)(2,1)S(1)} collective-permute-done((bf16[64,512]{1,0:T(8,128)(2,1)S(1)}, bf16[64,512]{1,0:T(8,128)(2,1)S(1)}, u32[]{:S(2)}, u32[]{:S(2)}) %collective-permute-start.14) | collective-permute-done | bytes 65568 | tf_op jit(solution)/shard_map/ppermute | solution.py:42
  100.7 1.6 %collective-permute-start.15 = (f32[64,512]{1,0:T(8,128)S(1)}, f32[64,512]{1,0:T(8,128)S(1)}, u32[]{:S(2)}, u32[]{:S(2)}) collective-permute-start(f32[64,512]{1,0:T(8,128)S(1)} %convert_add_fusion.mine_ref), channel_id=1, source_target_pairs={{0,1},{1,0},{2,3},{3,2},{4,5},{5,4},{6,7},{7,6},{8,9},{9,8},{10,11... | collective-permute-start | bytes 393224 | tf_op jit(solution)/shard_map/ppermute | solution.py:42
  102.2 1.5 %shard_map.102 = (f32[1016,128]{1,0:T(8,128)}, f32[32,128]{1,0:T(8,128)}) custom-call(s32[3]{0:T(128)S(1)} %pad_add_fusion.s_ref._, f32[2,128,512]{2,1,0:T(8,128)S(1)} %get-tuple-element.24.sums_ref, bf16[32,32,128]{2,1,0:T(8,128)(2,1)S(1)} %bitcast.21), custom_call_target="tpu_custom_call" | custom-call | bytes 1323008 | tf_op jit(solution)/shard_map/pallas_call | solution.py:27
  103.7 1.3 %shard_map.103 = f32[64,2,508]{2,1,0:T(2,128)} custom-call(s32[3]{0:T(128)S(1)} %pad_add_fusion.s_ref._, f32[64,512]{1,0:T(8,128)S(1)} %convert_add_fusion.mine_ref, f32[64,512]{1,0:T(8,128)S(1)} %collective-permute-done.15.theirs_ref), custom_call_target="tpu_custom_call" | custom-call | bytes 522240 | tf_op jit(solution)/shard_map/pallas_call | solution.py:27
  (42 shorter events, 9.3 us)
Async XLA Ops:
  0.6 15.8 %copy-start.1 = (f32[128]{0:T(128)S(1)}, f32[128]{0:T(128)}, u32[]{:S(2)}) copy-start(f32[128]{0:T(128)} %param.13) | copy-start | bytes 1540
  0.6 29.2 %copy-start.4 = (bf16[128,64]{0,1:T(8,128)(2,1)S(1)}, bf16[128,64]{0,1:T(8,128)(2,1)}, u32[]{:S(2)}) copy-start(bf16[128,64]{0,1:T(8,128)(2,1)} %param.12) | copy-start | bytes 49156
  0.7 33.3 %copy-start.3 = (bf16[64,2,508]{2,1,0:T(2,128)(2,1)S(1)}, bf16[64,2,508]{2,1,0:T(2,128)(2,1)}, u32[]{:S(2)}) copy-start(bf16[64,2,508]{2,1,0:T(2,128)(2,1)} %param.11) | copy-start | bytes 390148
  0.7 33.3 %copy-start = (s32[1,512]{1,0:T(1,128)S(1)}, s32[1,512]{1,0:T(1,128)}, u32[]{:S(2)}) copy-start(s32[1,512]{1,0:T(1,128)} %param.10) | copy-start | bytes 6148
  0.7 33.3 %copy-start.2 = (f32[32]{0:T(128)S(1)}, f32[32]{0:T(128)}, u32[]{:S(2)}) copy-start(f32[32]{0:T(128)} %temp_ref.1) | copy-start | bytes 388
  4.4 21.7 %all-to-all-start = ((bf16[32,32,128]{2,1,0:T(8,128)(2,1)}), bf16[32,32,128]{2,1,0:T(8,128)(2,1)S(1)}, u32[]{:S(2)}, u32[]{:S(2)}) async-start(bf16[32,32,128]{2,1,0:T(8,128)(2,1)} %bitcast.24), calls=%async_computation | async-start | bytes 524288 | tf_op jit(solution)/shard_map/all_to_all | solution.py:288
  26.1 13.4 %collective-permute-start = (bf16[32,32,128]{2,1,0:T(8,128)(2,1)S(1)}, bf16[32,32,128]{2,1,0:T(8,128)(2,1)S(1)}, u32[]{:S(2)}, u32[]{:S(2)}) collective-permute-start(bf16[32,32,128]{2,1,0:T(8,128)(2,1)S(1)} %all-to-all-done.own_ref.refs_0_), channel_id=1, source_target_pairs={{0,1},{1,0},{2,3},{3,2},{4,5},{5,4},{6,7},{7,6},{8,9},{9,8},{10,11... | collective-permute-start | bytes 786440 | tf_op jit(solution)/shard_map/ppermute | solution.py:42
  29.9 5.3 %collective-permute-start.1 = (bf16[80,128]{1,0:T(8,128)(2,1)S(1)}, bf16[80,128]{1,0:T(8,128)(2,1)S(1)}, u32[]{:S(2)}, u32[]{:S(2)}) collective-permute-start(bf16[80,128]{1,0:T(8,128)(2,1)S(1)} %pad_maximum_fusion.1.packed_ref), channel_id=1, source_target_pairs={{0,2},{2,0},{4,6},{6,4},{1,3},{3,1},{5,7},{7,5},{8,10},{10,8},{12,... | collective-permute-start | bytes 61448 | tf_op jit(solution)/shard_map/ppermute | solution.py:42
  31.2 4.3 %collective-permute-start.2 = (bf16[80,128]{1,0:T(8,128)(2,1)S(1)}, bf16[80,128]{1,0:T(8,128)(2,1)S(1)}, u32[]{:S(2)}, u32[]{:S(2)}) collective-permute-start(bf16[80,128]{1,0:T(8,128)(2,1)S(1)} %pad_maximum_fusion.1.packed_ref), channel_id=1, source_target_pairs={{0,4},{2,6},{4,0},{6,2},{1,5},{3,7},{5,1},{7,3},{8,12},{10,14},{12... | collective-permute-start | bytes 61448 | tf_op jit(solution)/shard_map/ppermute | solution.py:42
  33.6 3.8 %collective-permute-start.3 = (bf16[80,128]{1,0:T(8,128)(2,1)S(1)}, bf16[80,128]{1,0:T(8,128)(2,1)S(1)}, u32[]{:S(2)}, u32[]{:S(2)}) collective-permute-start(bf16[80,128]{1,0:T(8,128)(2,1)S(1)} %pad_maximum_fusion.1.packed_ref), channel_id=1, source_target_pairs={{0,6},{2,4},{4,2},{6,0},{1,7},{3,5},{5,3},{7,1},{8,14},{10,12},{12... | collective-permute-start | bytes 61448 | tf_op jit(solution)/shard_map/ppermute | solution.py:42
  58.5 8.9 %collective-permute-start.4 = (f32[2,8,128]{2,1,0:T(8,128)S(1)}, f32[2,8,128]{2,1,0:T(8,128)S(1)}, u32[]{:S(2)}, u32[]{:S(2)}) collective-permute-start(f32[2,8,128]{2,1,0:T(8,128)S(1)} %get-tuple-element.23.mine_ref), channel_id=1, source_target_pairs={{0,1},{1,0},{2,3},{3,2},{4,5},{5,4},{6,7},{7,6},{8,9},{9,8},{10,11... | collective-permute-start | bytes 24584 | tf_op jit(solution)/shard_map/ppermute | solution.py:42
  63.6 12.2 %collective-permute-start.7 = (bf16[32,32,128]{2,1,0:T(8,128)(2,1)S(1)}, bf16[32,32,128]{2,1,0:T(8,128)(2,1)S(1)}, u32[]{:S(2)}, u32[]{:S(2)}) collective-permute-start(bf16[32,32,128]{2,1,0:T(8,128)(2,1)S(1)} %all-to-all-done.own_ref.refs_0_), channel_id=1, source_target_pairs={{0,6},{2,4},{4,2},{6,0},{1,7},{3,5},{5,3},{7,1},{8,14},{10,12},{12... | collective-permute-start | bytes 786440 | tf_op jit(solution)/shard_map/ppermute | solution.py:42
  64.1 13.0 %collective-permute-start.5 = (bf16[32,32,128]{2,1,0:T(8,128)(2,1)S(1)}, bf16[32,32,128]{2,1,0:T(8,128)(2,1)S(1)}, u32[]{:S(2)}, u32[]{:S(2)}) collective-permute-start(bf16[32,32,128]{2,1,0:T(8,128)(2,1)S(1)} %all-to-all-done.own_ref.refs_0_), channel_id=1, source_target_pairs={{0,2},{2,0},{4,6},{6,4},{1,3},{3,1},{5,7},{7,5},{8,10},{10,8},{12,... | collective-permute-start | bytes 786440 | tf_op jit(solution)/shard_map/ppermute | solution.py:42
  64.1 15.0 %collective-permute-start.6 = (bf16[32,32,128]{2,1,0:T(8,128)(2,1)S(1)}, bf16[32,32,128]{2,1,0:T(8,128)(2,1)S(1)}, u32[]{:S(2)}, u32[]{:S(2)}) collective-permute-start(bf16[32,32,128]{2,1,0:T(8,128)(2,1)S(1)} %all-to-all-done.own_ref.refs_0_), channel_id=1, source_target_pairs={{0,4},{2,6},{4,0},{6,2},{1,5},{3,7},{5,1},{7,3},{8,12},{10,14},{12... | collective-permute-start | bytes 786440 | tf_op jit(solution)/shard_map/ppermute | solution.py:42
  68.7 19.1 %all-to-all-start.2 = ((bf16[128,8,128]{2,1,0:T(8,128)(2,1)}), bf16[128,8,128]{2,1,0:T(8,128)(2,1)S(1)}, u32[]{:S(2)}, u32[]{:S(2)}) async-start(bf16[128,8,128]{2,1,0:T(8,128)(2,1)} %bitcast.10), calls=%async_computation.2 | async-start | bytes 524288 | tf_op jit(solution)/shard_map/all_to_all | solution.py:349
  75.8 5.7 %collective-permute-start.10 = (bf16[32,32,128]{2,1,0:T(8,128)(2,1)S(1)}, bf16[32,32,128]{2,1,0:T(8,128)(2,1)S(1)}, u32[]{:S(2)}, u32[]{:S(2)}) collective-permute-start(bf16[32,32,128]{2,1,0:T(8,128)(2,1)S(1)} %collective-permute-done.7.refs_3_), channel_id=1, source_target_pairs={{0,1},{1,0},{2,3},{3,2},{4,5},{5,4},{6,7},{7,6},{8,9},{9,8},{10,11... | collective-permute-start | bytes 786440 | tf_op jit(solution)/shard_map/ppermute | solution.py:42
  77.1 4.4 %collective-permute-start.8 = (bf16[32,32,128]{2,1,0:T(8,128)(2,1)S(1)}, bf16[32,32,128]{2,1,0:T(8,128)(2,1)S(1)}, u32[]{:S(2)}, u32[]{:S(2)}) collective-permute-start(bf16[32,32,128]{2,1,0:T(8,128)(2,1)S(1)} %collective-permute-done.5.refs_1_), channel_id=1, source_target_pairs={{0,1},{1,0},{2,3},{3,2},{4,5},{5,4},{6,7},{7,6},{8,9},{9,8},{10,11... | collective-permute-start | bytes 786440 | tf_op jit(solution)/shard_map/ppermute | solution.py:42
  79.1 2.7 %collective-permute-start.9 = (bf16[32,32,128]{2,1,0:T(8,128)(2,1)S(1)}, bf16[32,32,128]{2,1,0:T(8,128)(2,1)S(1)}, u32[]{:S(2)}, u32[]{:S(2)}) collective-permute-start(bf16[32,32,128]{2,1,0:T(8,128)(2,1)S(1)} %collective-permute-done.6.refs_2_), channel_id=1, source_target_pairs={{0,1},{1,0},{2,3},{3,2},{4,5},{5,4},{6,7},{7,6},{8,9},{9,8},{10,11... | collective-permute-start | bytes 786440 | tf_op jit(solution)/shard_map/ppermute | solution.py:42
  89.4 4.5 %collective-permute-start.11 = (bf16[64,512]{1,0:T(8,128)(2,1)S(1)}, bf16[64,512]{1,0:T(8,128)(2,1)S(1)}, u32[]{:S(2)}, u32[]{:S(2)}) collective-permute-start(bf16[64,512]{1,0:T(8,128)(2,1)S(1)} %get-tuple-element.28), channel_id=1, source_target_pairs={{0,1},{1,0},{2,3},{3,2},{4,5},{5,4},{6,7},{7,6},{8,9},{9,8},{10,11... | collective-permute-start | bytes 196616 | tf_op jit(solution)/shard_map/ppermute | solution.py:42
  94.0 3.9 %collective-permute-start.12 = (bf16[64,512]{1,0:T(8,128)(2,1)S(1)}, bf16[64,512]{1,0:T(8,128)(2,1)S(1)}, u32[]{:S(2)}, u32[]{:S(2)}) collective-permute-start(bf16[64,512]{1,0:T(8,128)(2,1)S(1)} %add_convert_fusion), channel_id=1, source_target_pairs={{0,2},{2,0},{4,6},{6,4},{1,3},{3,1},{5,7},{7,5},{8,10},{10,8},{12,... | collective-permute-start | bytes 196616 | tf_op jit(solution)/shard_map/ppermute | solution.py:42
  94.2 4.7 %collective-permute-start.13 = (bf16[64,512]{1,0:T(8,128)(2,1)S(1)}, bf16[64,512]{1,0:T(8,128)(2,1)S(1)}, u32[]{:S(2)}, u32[]{:S(2)}) collective-permute-start(bf16[64,512]{1,0:T(8,128)(2,1)S(1)} %add_convert_fusion), channel_id=1, source_target_pairs={{0,4},{2,6},{4,0},{6,2},{1,5},{3,7},{5,1},{7,3},{8,12},{10,14},{12... | collective-permute-start | bytes 196616 | tf_op jit(solution)/shard_map/ppermute | solution.py:42
  95.7 4.9 %collective-permute-start.14 = (bf16[64,512]{1,0:T(8,128)(2,1)S(1)}, bf16[64,512]{1,0:T(8,128)(2,1)S(1)}, u32[]{:S(2)}, u32[]{:S(2)}) collective-permute-start(bf16[64,512]{1,0:T(8,128)(2,1)S(1)} %add_convert_fusion), channel_id=1, source_target_pairs={{0,6},{2,4},{4,2},{6,0},{1,7},{3,5},{5,3},{7,1},{8,14},{10,12},{12... | collective-permute-start | bytes 196616 | tf_op jit(solution)/shard_map/ppermute | solution.py:42
  100.7 3.1 %collective-permute-start.15 = (f32[64,512]{1,0:T(8,128)S(1)}, f32[64,512]{1,0:T(8,128)S(1)}, u32[]{:S(2)}, u32[]{:S(2)}) collective-permute-start(f32[64,512]{1,0:T(8,128)S(1)} %convert_add_fusion.mine_ref), channel_id=1, source_target_pairs={{0,1},{1,0},{2,3},{3,2},{4,5},{5,4},{6,7},{7,6},{8,9},{9,8},{10,11... | collective-permute-start | bytes 393224 | tf_op jit(solution)/shard_map/ppermute | solution.py:42

commit v3 on v2

--- a/solution.py
+++ b/solution.py
@@ -50,7 +50,7 @@
 def rotate_and_cut(width, parts):
     tiles = -(-width // LANES)
 
-    def kernel(shifts_ref, images_ref, out_ref, block, sems):
+    def kernel(shifts_ref, images_ref, out_ref, block, sems, spread):
         c, x = lax.axis_index("c"), lax.axis_index("x")
         whole = images_ref.shape[2] // LANES
         bounds = [whole * k // CUTS for k in range(CUTS + 1)]
@@ -76,8 +76,13 @@
         for k in range(CUTS):
             copies[k].wait()
             for tile in range(bounds[k], bounds[k + 1]):
-                both = block[:, :, tile * LANES : (tile + 1) * LANES].astype(jnp.float32)
-                turned.append(both[:, 0, :] * a + both[:, 1, :] * b)
+                at = slice(tile * LANES, (tile + 1) * LANES)
+                for n in range(ROWS):
+                    spread[tile, 2 * n : 2 * n + 2, :] = block[n, :, at].astype(jnp.float32)
+            for tile in range(bounds[k], bounds[k + 1]):
+                at = slice(tile * LANES, (tile + 1) * LANES)
+                first, second = (spread[tile, pl.ds(p, ROWS, stride=2), :] for p in range(2))
+                turned.append(first * a + second * b)
             while part < parts and (part + 1) * width <= len(turned) * LANES:
                 shift = (part * width) % LANES
                 for t in range(tiles):
@@ -103,7 +108,7 @@
         out_shape=shape((parts, tiles, ROWS, LANES), jnp.bfloat16),
         in_specs=[pl.BlockSpec(memory_space=pltpu.SMEM), pl.BlockSpec(memory_space=pl.ANY)],
         out_specs=pl.BlockSpec(memory_space=pltpu.VMEM),
-        scratch_shapes=[pltpu.VMEM((ROWS, 2, images.shape[2]), jnp.bfloat16), pltpu.SemaphoreType.DMA((CUTS,))],
+        scratch_shapes=[pltpu.VMEM((ROWS, 2, images.shape[2]), jnp.bfloat16), pltpu.SemaphoreType.DMA((CUTS,)), pltpu.VMEM((images.shape[2] // LANES, 2 * ROWS, LANES), jnp.float32)],
         compiler_params=pltpu.CompilerParams(vmem_limit_bytes=60 * 2**20),
     )(shifts, images)
 

time: 105 us -> 105 us (level)
  no operation moved by 1% of the time
where the time goes in v3:
time: 105 us
  starting transfers between devices  47.8 us (46%)
  waiting for transfers between devices  23.6 us (22%)
  blocking collectives  17 us (16%)
  Pallas kernels  15 us (14%)
    ppermute x16, starting transfers between devices, across(): lax.ppermute(x, axis, [(s, s ^ turn) for s in range(lax.axis_size(axis))])  28.7 us
    all_to_all x1, blocking collectives, shards(): partial = lax.all_to_all(partial, 'img', 0, 0, tiled=True)  17 us
    all_to_all x1, starting transfers between devices, shards(): lax.all_to_all(cut.reshape(groups, tiles * ROWS, LANES), 'img', 0, 0, til...  12 us
    pallas_call x9, Pallas kernels, call(): pl.pallas_call(kernel, out_shape=out_shape, in_specs=specs, out_specs=out...  11.9 us
    all_to_all x1, waiting for transfers between devices, shards(): lax.all_to_all(cut.reshape(groups, tiles * ROWS, LANES), 'img', 0, 0, til...  9.66 us
    ppermute x16, waiting for transfers between devices, across(): lax.ppermute(x, axis, [(s, s ^ turn) for s in range(lax.axis_size(axis))])  7.97 us
    all_to_all x1, starting transfers between devices, shards(): posts = lax.all_to_all(copies, ('img', 'x'), 0, 0, tiled=True)  7.07 us
    all_to_all x1, waiting for transfers between devices, shards(): posts = lax.all_to_all(copies, ('img', 'x'), 0, 0, tiled=True)  6.01 us
  transfers between devices with their start and end apart: 18, of which 9 were waited for; matrix products, arithmetic and copies ran while one was open for 0% of the time, Pallas kernels for 7%

profile of v3, /device:TPU:1, one launch (start us, length us, event | category | flops | bytes accessed | tf_op | source)
XLA Modules:
  0.0 104.5 jit_solution(16712376732662898830)
XLA Ops:
  0.7 3.2 %shard_map.94 = bf16[32,4,8,128]{3,2,1,0:T(8,128)(2,1)} custom-call(s32[32]{0:T(128)} %shifts_ref.1, bf16[32,2,16256]{2,1,0:T(2,128)(2,1)} %images_ref.1), custom_call_target="tpu_custom_call" | custom-call | tf_op jit(solution)/shard_map/pallas_call | solution.py:106
  3.9 12.0 %all-to-all-start = ((bf16[32,32,128]{2,1,0:T(8,128)(2,1)}), bf16[32,32,128]{2,1,0:T(8,128)(2,1)S(1)}, u32[]{:S(2)}, u32[]{:S(2)}) async-start(bf16[32,32,128]{2,1,0:T(8,128)(2,1)} %bitcast.24), calls=%async_computation | async-start | bytes 524288 | tf_op jit(solution)/shard_map/all_to_all | solution.py:293
  15.9 9.7 %all-to-all-done.own_ref.refs_0_ = bf16[32,32,128]{2,1,0:T(8,128)(2,1)S(1)} async-done(((bf16[32,32,128]{2,1,0:T(8,128)(2,1)}), bf16[32,32,128]{2,1,0:T(8,128)(2,1)S(1)}, u32[]{:S(2)}, u32[]{:S(2)}) %all-to-all-start) | async-done | bytes 262176 | tf_op jit(solution)/shard_map/all_to_all | solution.py:293
  25.6 3.7 %collective-permute-start = (bf16[32,32,128]{2,1,0:T(8,128)(2,1)S(1)}, bf16[32,32,128]{2,1,0:T(8,128)(2,1)S(1)}, u32[]{:S(2)}, u32[]{:S(2)}) collective-permute-start(bf16[32,32,128]{2,1,0:T(8,128)(2,1)S(1)} %all-to-all-done.own_ref.refs_0_), channel_id=1, source_target_pairs={{0,1},{1,0},{2,3},{3,2},{4,5},{5,4},{6,7},{7,6},{8,9},{9,8},{10,11... | collective-permute-start | bytes 786440 | tf_op jit(solution)/shard_map/ppermute | solution.py:42
  29.3 1.3 %collective-permute-start.1 = (bf16[80,128]{1,0:T(8,128)(2,1)S(1)}, bf16[80,128]{1,0:T(8,128)(2,1)S(1)}, u32[]{:S(2)}, u32[]{:S(2)}) collective-permute-start(bf16[80,128]{1,0:T(8,128)(2,1)S(1)} %pad_maximum_fusion.1.packed_ref), channel_id=1, source_target_pairs={{0,2},{2,0},{4,6},{6,4},{1,3},{3,1},{5,7},{7,5},{8,10},{10,8},{12,... | collective-permute-start | bytes 61448 | tf_op jit(solution)/shard_map/ppermute | solution.py:42
  30.6 2.5 %collective-permute-start.2 = (bf16[80,128]{1,0:T(8,128)(2,1)S(1)}, bf16[80,128]{1,0:T(8,128)(2,1)S(1)}, u32[]{:S(2)}, u32[]{:S(2)}) collective-permute-start(bf16[80,128]{1,0:T(8,128)(2,1)S(1)} %pad_maximum_fusion.1.packed_ref), channel_id=1, source_target_pairs={{0,4},{2,6},{4,0},{6,2},{1,5},{3,7},{5,1},{7,3},{8,12},{10,14},{12... | collective-permute-start | bytes 61448 | tf_op jit(solution)/shard_map/ppermute | solution.py:42
  34.9 2.0 %collective-permute-done.3.refs_2_ = bf16[80,128]{1,0:T(8,128)(2,1)S(1)} collective-permute-done((bf16[80,128]{1,0:T(8,128)(2,1)S(1)}, bf16[80,128]{1,0:T(8,128)(2,1)S(1)}, u32[]{:S(2)}, u32[]{:S(2)}) %collective-permute-start.3) | collective-permute-done | bytes 20512 | tf_op jit(solution)/shard_map/ppermute | solution.py:42
  36.9 2.0 %shard_map.96 = (bf16[3,2,128,512]{3,2,1,0:T(8,128)(2,1)S(1)}, f32[3,128]{1,0:T(4,128)S(1)}) custom-call(s32[3]{0:T(128)S(1)} %pad_add_fusion.s_ref._, bf16[2,64,512]{2,1,0:T(8,128)(2,1)S(1)} %pad.9.volume_ref, bf16[80,128]{1,0:T(8,128)(2,1)S(1)} %collective-permute-done.1.refs_0_, bf16[80,128]{1,0:T(8,128)(2,1)S(1)} %collective-permute-done.2.refs_1_, ...), custom_call_target="tpu_custom_call" | custom-call | flops 50331648 | bytes 980480 | tf_op jit(solution)/shard_map/pallas_call | solution.py:27
  40.2 17.0 %all_to_all.15.parts_ref = f32[32,32,128]{2,1,0:T(8,128)S(1)} all-to-all(f32[32,32,128]{2,1,0:T(8,128)S(1)} %shard_map.97), channel_id=1, replica_groups=mesh['img'=32,'x'=4,'c'=2] {'img'}, dimensions={0} | all-to-all | bytes 1048576 | tf_op jit(solution)/shard_map/all_to_all | solution.py:339
  58.0 5.1 %collective-permute-start.4 = (f32[2,8,128]{2,1,0:T(8,128)S(1)}, f32[2,8,128]{2,1,0:T(8,128)S(1)}, u32[]{:S(2)}, u32[]{:S(2)}) collective-permute-start(f32[2,8,128]{2,1,0:T(8,128)S(1)} %get-tuple-element.23.mine_ref), channel_id=1, source_target_pairs={{0,1},{1,0},{2,3},{3,2},{4,5},{5,4},{6,7},{7,6},{8,9},{9,8},{10,11... | collective-permute-start | bytes 24584 | tf_op jit(solution)/shard_map/ppermute | solution.py:42
  63.6 3.3 %collective-permute-start.6 = (bf16[32,32,128]{2,1,0:T(8,128)(2,1)S(1)}, bf16[32,32,128]{2,1,0:T(8,128)(2,1)S(1)}, u32[]{:S(2)}, u32[]{:S(2)}) collective-permute-start(bf16[32,32,128]{2,1,0:T(8,128)(2,1)S(1)} %all-to-all-done.own_ref.refs_0_), channel_id=1, source_target_pairs={{0,4},{2,6},{4,0},{6,2},{1,5},{3,7},{5,1},{7,3},{8,12},{10,14},{12... | collective-permute-start | bytes 786440 | tf_op jit(solution)/shard_map/ppermute | solution.py:42
  68.2 7.1 %all-to-all-start.2 = ((bf16[128,8,128]{2,1,0:T(8,128)(2,1)}), bf16[128,8,128]{2,1,0:T(8,128)(2,1)S(1)}, u32[]{:S(2)}, u32[]{:S(2)}) async-start(bf16[128,8,128]{2,1,0:T(8,128)(2,1)} %bitcast.10), calls=%async_computation.2 | async-start | bytes 524288 | tf_op jit(solution)/shard_map/all_to_all | solution.py:354
  75.3 1.3 %collective-permute-start.10 = (bf16[32,32,128]{2,1,0:T(8,128)(2,1)S(1)}, bf16[32,32,128]{2,1,0:T(8,128)(2,1)S(1)}, u32[]{:S(2)}, u32[]{:S(2)}) collective-permute-start(bf16[32,32,128]{2,1,0:T(8,128)(2,1)S(1)} %collective-permute-done.7.refs_3_), channel_id=1, source_target_pairs={{0,1},{1,0},{2,3},{3,2},{4,5},{5,4},{6,7},{7,6},{8,9},{9,8},{10,11... | collective-permute-start | bytes 786440 | tf_op jit(solution)/shard_map/ppermute | solution.py:42
  76.7 1.8 %collective-permute-done.6.refs_2_ = bf16[32,32,128]{2,1,0:T(8,128)(2,1)S(1)} collective-permute-done((bf16[32,32,128]{2,1,0:T(8,128)(2,1)S(1)}, bf16[32,32,128]{2,1,0:T(8,128)(2,1)S(1)}, u32[]{:S(2)}, u32[]{:S(2)}) %collective-permute-start.6) | collective-permute-done | bytes 262176 | tf_op jit(solution)/shard_map/ppermute | solution.py:42
  78.5 1.6 %collective-permute-start.9 = (bf16[32,32,128]{2,1,0:T(8,128)(2,1)S(1)}, bf16[32,32,128]{2,1,0:T(8,128)(2,1)S(1)}, u32[]{:S(2)}, u32[]{:S(2)}) collective-permute-start(bf16[32,32,128]{2,1,0:T(8,128)(2,1)S(1)} %collective-permute-done.6.refs_2_), channel_id=1, source_target_pairs={{0,1},{1,0},{2,3},{3,2},{4,5},{5,4},{6,7},{7,6},{8,9},{9,8},{10,11... | collective-permute-start | bytes 786440 | tf_op jit(solution)/shard_map/ppermute | solution.py:42
  81.3 6.0 %all-to-all-done.2 = bf16[128,8,128]{2,1,0:T(8,128)(2,1)S(1)} async-done(((bf16[128,8,128]{2,1,0:T(8,128)(2,1)}), bf16[128,8,128]{2,1,0:T(8,128)(2,1)S(1)}, u32[]{:S(2)}, u32[]{:S(2)}) %all-to-all-start.2) | async-done | bytes 262176 | tf_op jit(solution)/shard_map/all_to_all | solution.py:354
  87.3 1.6 %shard_map.101 = (f32[2,128,512]{2,1,0:T(8,128)S(1)}, f32[64,512]{1,0:T(8,128)S(1)}, bf16[64,512]{1,0:T(8,128)(2,1)S(1)}) custom-call(s32[3]{0:T(128)S(1)} %pad_add_fusion.s_ref._, bf16[32,4,8,128]{3,2,1,0:T(8,128)(2,1)S(1)} %bitcast.20, bf16[2,128,512]{2,1,0:T(8,128)(2,1)S(1)} %get-tuple-element.16.near_ref.slices_ref, ...), custom_call_target="tpu_custom_call" | custom-call | flops 268435456 | bytes 3506176 | tf_op jit(solution)/shard_map/pallas_call | solution.py:27
  88.9 3.6 %collective-permute-start.11 = (bf16[64,512]{1,0:T(8,128)(2,1)S(1)}, bf16[64,512]{1,0:T(8,128)(2,1)S(1)}, u32[]{:S(2)}, u32[]{:S(2)}) collective-permute-start(bf16[64,512]{1,0:T(8,128)(2,1)S(1)} %get-tuple-element.28), channel_id=1, source_target_pairs={{0,1},{1,0},{2,3},{3,2},{4,5},{5,4},{6,7},{7,6},{8,9},{9,8},{10,11... | collective-permute-start | bytes 196616 | tf_op jit(solution)/shard_map/ppermute | solution.py:42
  93.7 1.5 %collective-permute-start.13 = (bf16[64,512]{1,0:T(8,128)(2,1)S(1)}, bf16[64,512]{1,0:T(8,128)(2,1)S(1)}, u32[]{:S(2)}, u32[]{:S(2)}) collective-permute-start(bf16[64,512]{1,0:T(8,128)(2,1)S(1)} %add_convert_fusion), channel_id=1, source_target_pairs={{0,4},{2,6},{4,0},{6,2},{1,5},{3,7},{5,1},{7,3},{8,12},{10,14},{12... | collective-permute-start | bytes 196616 | tf_op jit(solution)/shard_map/ppermute | solution.py:42
  95.2 2.2 %collective-permute-start.14 = (bf16[64,512]{1,0:T(8,128)(2,1)S(1)}, bf16[64,512]{1,0:T(8,128)(2,1)S(1)}, u32[]{:S(2)}, u32[]{:S(2)}) collective-permute-start(bf16[64,512]{1,0:T(8,128)(2,1)S(1)} %add_convert_fusion), channel_id=1, source_target_pairs={{0,6},{2,4},{4,2},{6,0},{1,7},{3,5},{5,3},{7,1},{8,14},{10,12},{12... | collective-permute-start | bytes 196616 | tf_op jit(solution)/shard_map/ppermute | solution.py:42
  98.3 1.7 %collective-permute-done.14 = bf16[64,512]{1,0:T(8,128)(2,1)S(1)} collective-permute-done((bf16[64,512]{1,0:T(8,128)(2,1)S(1)}, bf16[64,512]{1,0:T(8,128)(2,1)S(1)}, u32[]{:S(2)}, u32[]{:S(2)}) %collective-permute-start.14) | collective-permute-done | bytes 65568 | tf_op jit(solution)/shard_map/ppermute | solution.py:42
  100.1 1.6 %collective-permute-start.15 = (f32[64,512]{1,0:T(8,128)S(1)}, f32[64,512]{1,0:T(8,128)S(1)}, u32[]{:S(2)}, u32[]{:S(2)}) collective-permute-start(f32[64,512]{1,0:T(8,128)S(1)} %convert_add_fusion.mine_ref), channel_id=1, source_target_pairs={{0,1},{1,0},{2,3},{3,2},{4,5},{5,4},{6,7},{7,6},{8,9},{9,8},{10,11... | collective-permute-start | bytes 393224 | tf_op jit(solution)/shard_map/ppermute | solution.py:42
  101.7 1.5 %shard_map.102 = (f32[1016,128]{1,0:T(8,128)}, f32[32,128]{1,0:T(8,128)}) custom-call(s32[3]{0:T(128)S(1)} %pad_add_fusion.s_ref._, f32[2,128,512]{2,1,0:T(8,128)S(1)} %get-tuple-element.24.sums_ref, bf16[32,32,128]{2,1,0:T(8,128)(2,1)S(1)} %bitcast.21), custom_call_target="tpu_custom_call" | custom-call | bytes 1323008 | tf_op jit(solution)/shard_map/pallas_call | solution.py:27
  103.2 1.3 %shard_map.103 = f32[64,2,508]{2,1,0:T(2,128)} custom-call(s32[3]{0:T(128)S(1)} %pad_add_fusion.s_ref._, f32[64,512]{1,0:T(8,128)S(1)} %convert_add_fusion.mine_ref, f32[64,512]{1,0:T(8,128)S(1)} %collective-permute-done.15.theirs_ref), custom_call_target="tpu_custom_call" | custom-call | bytes 522240 | tf_op jit(solution)/shard_map/pallas_call | solution.py:27
  (42 shorter events, 9.1 us)
Async XLA Ops:
  0.6 15.3 %copy-start.1 = (f32[128]{0:T(128)S(1)}, f32[128]{0:T(128)}, u32[]{:S(2)}) copy-start(f32[128]{0:T(128)} %param.13) | copy-start | bytes 1540
  0.6 28.7 %copy-start.4 = (bf16[128,64]{0,1:T(8,128)(2,1)S(1)}, bf16[128,64]{0,1:T(8,128)(2,1)}, u32[]{:S(2)}) copy-start(bf16[128,64]{0,1:T(8,128)(2,1)} %param.12) | copy-start | bytes 49156
  0.7 32.7 %copy-start.3 = (bf16[64,2,508]{2,1,0:T(2,128)(2,1)S(1)}, bf16[64,2,508]{2,1,0:T(2,128)(2,1)}, u32[]{:S(2)}) copy-start(bf16[64,2,508]{2,1,0:T(2,128)(2,1)} %param.11) | copy-start | bytes 390148
  0.7 32.7 %copy-start = (s32[1,512]{1,0:T(1,128)S(1)}, s32[1,512]{1,0:T(1,128)}, u32[]{:S(2)}) copy-start(s32[1,512]{1,0:T(1,128)} %param.10) | copy-start | bytes 6148
  0.7 32.7 %copy-start.2 = (f32[32]{0:T(128)S(1)}, f32[32]{0:T(128)}, u32[]{:S(2)}) copy-start(f32[32]{0:T(128)} %temp_ref.1) | copy-start | bytes 388
  3.9 21.7 %all-to-all-start = ((bf16[32,32,128]{2,1,0:T(8,128)(2,1)}), bf16[32,32,128]{2,1,0:T(8,128)(2,1)S(1)}, u32[]{:S(2)}, u32[]{:S(2)}) async-start(bf16[32,32,128]{2,1,0:T(8,128)(2,1)} %bitcast.24), calls=%async_computation | async-start | bytes 524288 | tf_op jit(solution)/shard_map/all_to_all | solution.py:293
  25.6 13.4 %collective-permute-start = (bf16[32,32,128]{2,1,0:T(8,128)(2,1)S(1)}, bf16[32,32,128]{2,1,0:T(8,128)(2,1)S(1)}, u32[]{:S(2)}, u32[]{:S(2)}) collective-permute-start(bf16[32,32,128]{2,1,0:T(8,128)(2,1)S(1)} %all-to-all-done.own_ref.refs_0_), channel_id=1, source_target_pairs={{0,1},{1,0},{2,3},{3,2},{4,5},{5,4},{6,7},{7,6},{8,9},{9,8},{10,11... | collective-permute-start | bytes 786440 | tf_op jit(solution)/shard_map/ppermute | solution.py:42
  29.3 5.3 %collective-permute-start.1 = (bf16[80,128]{1,0:T(8,128)(2,1)S(1)}, bf16[80,128]{1,0:T(8,128)(2,1)S(1)}, u32[]{:S(2)}, u32[]{:S(2)}) collective-permute-start(bf16[80,128]{1,0:T(8,128)(2,1)S(1)} %pad_maximum_fusion.1.packed_ref), channel_id=1, source_target_pairs={{0,2},{2,0},{4,6},{6,4},{1,3},{3,1},{5,7},{7,5},{8,10},{10,8},{12,... | collective-permute-start | bytes 61448 | tf_op jit(solution)/shard_map/ppermute | solution.py:42
  30.6 4.3 %collective-permute-start.2 = (bf16[80,128]{1,0:T(8,128)(2,1)S(1)}, bf16[80,128]{1,0:T(8,128)(2,1)S(1)}, u32[]{:S(2)}, u32[]{:S(2)}) collective-permute-start(bf16[80,128]{1,0:T(8,128)(2,1)S(1)} %pad_maximum_fusion.1.packed_ref), channel_id=1, source_target_pairs={{0,4},{2,6},{4,0},{6,2},{1,5},{3,7},{5,1},{7,3},{8,12},{10,14},{12... | collective-permute-start | bytes 61448 | tf_op jit(solution)/shard_map/ppermute | solution.py:42
  33.1 3.8 %collective-permute-start.3 = (bf16[80,128]{1,0:T(8,128)(2,1)S(1)}, bf16[80,128]{1,0:T(8,128)(2,1)S(1)}, u32[]{:S(2)}, u32[]{:S(2)}) collective-permute-start(bf16[80,128]{1,0:T(8,128)(2,1)S(1)} %pad_maximum_fusion.1.packed_ref), channel_id=1, source_target_pairs={{0,6},{2,4},{4,2},{6,0},{1,7},{3,5},{5,3},{7,1},{8,14},{10,12},{12... | collective-permute-start | bytes 61448 | tf_op jit(solution)/shard_map/ppermute | solution.py:42
  58.0 8.9 %collective-permute-start.4 = (f32[2,8,128]{2,1,0:T(8,128)S(1)}, f32[2,8,128]{2,1,0:T(8,128)S(1)}, u32[]{:S(2)}, u32[]{:S(2)}) collective-permute-start(f32[2,8,128]{2,1,0:T(8,128)S(1)} %get-tuple-element.23.mine_ref), channel_id=1, source_target_pairs={{0,1},{1,0},{2,3},{3,2},{4,5},{5,4},{6,7},{7,6},{8,9},{9,8},{10,11... | collective-permute-start | bytes 24584 | tf_op jit(solution)/shard_map/ppermute | solution.py:42
  63.0 12.2 %collective-permute-start.7 = (bf16[32,32,128]{2,1,0:T(8,128)(2,1)S(1)}, bf16[32,32,128]{2,1,0:T(8,128)(2,1)S(1)}, u32[]{:S(2)}, u32[]{:S(2)}) collective-permute-start(bf16[32,32,128]{2,1,0:T(8,128)(2,1)S(1)} %all-to-all-done.own_ref.refs_0_), channel_id=1, source_target_pairs={{0,6},{2,4},{4,2},{6,0},{1,7},{3,5},{5,3},{7,1},{8,14},{10,12},{12... | collective-permute-start | bytes 786440 | tf_op jit(solution)/shard_map/ppermute | solution.py:42
  63.6 13.0 %collective-permute-start.5 = (bf16[32,32,128]{2,1,0:T(8,128)(2,1)S(1)}, bf16[32,32,128]{2,1,0:T(8,128)(2,1)S(1)}, u32[]{:S(2)}, u32[]{:S(2)}) collective-permute-start(bf16[32,32,128]{2,1,0:T(8,128)(2,1)S(1)} %all-to-all-done.own_ref.refs_0_), channel_id=1, source_target_pairs={{0,2},{2,0},{4,6},{6,4},{1,3},{3,1},{5,7},{7,5},{8,10},{10,8},{12,... | collective-permute-start | bytes 786440 | tf_op jit(solution)/shard_map/ppermute | solution.py:42
  63.6 15.0 %collective-permute-start.6 = (bf16[32,32,128]{2,1,0:T(8,128)(2,1)S(1)}, bf16[32,32,128]{2,1,0:T(8,128)(2,1)S(1)}, u32[]{:S(2)}, u32[]{:S(2)}) collective-permute-start(bf16[32,32,128]{2,1,0:T(8,128)(2,1)S(1)} %all-to-all-done.own_ref.refs_0_), channel_id=1, source_target_pairs={{0,4},{2,6},{4,0},{6,2},{1,5},{3,7},{5,1},{7,3},{8,12},{10,14},{12... | collective-permute-start | bytes 786440 | tf_op jit(solution)/shard_map/ppermute | solution.py:42
  68.2 19.1 %all-to-all-start.2 = ((bf16[128,8,128]{2,1,0:T(8,128)(2,1)}), bf16[128,8,128]{2,1,0:T(8,128)(2,1)S(1)}, u32[]{:S(2)}, u32[]{:S(2)}) async-start(bf16[128,8,128]{2,1,0:T(8,128)(2,1)} %bitcast.10), calls=%async_computation.2 | async-start | bytes 524288 | tf_op jit(solution)/shard_map/all_to_all | solution.py:354
  75.3 5.7 %collective-permute-start.10 = (bf16[32,32,128]{2,1,0:T(8,128)(2,1)S(1)}, bf16[32,32,128]{2,1,0:T(8,128)(2,1)S(1)}, u32[]{:S(2)}, u32[]{:S(2)}) collective-permute-start(bf16[32,32,128]{2,1,0:T(8,128)(2,1)S(1)} %collective-permute-done.7.refs_3_), channel_id=1, source_target_pairs={{0,1},{1,0},{2,3},{3,2},{4,5},{5,4},{6,7},{7,6},{8,9},{9,8},{10,11... | collective-permute-start | bytes 786440 | tf_op jit(solution)/shard_map/ppermute | solution.py:42
  76.6 4.4 %collective-permute-start.8 = (bf16[32,32,128]{2,1,0:T(8,128)(2,1)S(1)}, bf16[32,32,128]{2,1,0:T(8,128)(2,1)S(1)}, u32[]{:S(2)}, u32[]{:S(2)}) collective-permute-start(bf16[32,32,128]{2,1,0:T(8,128)(2,1)S(1)} %collective-permute-done.5.refs_1_), channel_id=1, source_target_pairs={{0,1},{1,0},{2,3},{3,2},{4,5},{5,4},{6,7},{7,6},{8,9},{9,8},{10,11... | collective-permute-start | bytes 786440 | tf_op jit(solution)/shard_map/ppermute | solution.py:42
  78.5 2.7 %collective-permute-start.9 = (bf16[32,32,128]{2,1,0:T(8,128)(2,1)S(1)}, bf16[32,32,128]{2,1,0:T(8,128)(2,1)S(1)}, u32[]{:S(2)}, u32[]{:S(2)}) collective-permute-start(bf16[32,32,128]{2,1,0:T(8,128)(2,1)S(1)} %collective-permute-done.6.refs_2_), channel_id=1, source_target_pairs={{0,1},{1,0},{2,3},{3,2},{4,5},{5,4},{6,7},{7,6},{8,9},{9,8},{10,11... | collective-permute-start | bytes 786440 | tf_op jit(solution)/shard_map/ppermute | solution.py:42
  88.9 4.5 %collective-permute-start.11 = (bf16[64,512]{1,0:T(8,128)(2,1)S(1)}, bf16[64,512]{1,0:T(8,128)(2,1)S(1)}, u32[]{:S(2)}, u32[]{:S(2)}) collective-permute-start(bf16[64,512]{1,0:T(8,128)(2,1)S(1)} %get-tuple-element.28), channel_id=1, source_target_pairs={{0,1},{1,0},{2,3},{3,2},{4,5},{5,4},{6,7},{7,6},{8,9},{9,8},{10,11... | collective-permute-start | bytes 196616 | tf_op jit(solution)/shard_map/ppermute | solution.py:42
  93.4 3.9 %collective-permute-start.12 = (bf16[64,512]{1,0:T(8,128)(2,1)S(1)}, bf16[64,512]{1,0:T(8,128)(2,1)S(1)}, u32[]{:S(2)}, u32[]{:S(2)}) collective-permute-start(bf16[64,512]{1,0:T(8,128)(2,1)S(1)} %add_convert_fusion), channel_id=1, source_target_pairs={{0,2},{2,0},{4,6},{6,4},{1,3},{3,1},{5,7},{7,5},{8,10},{10,8},{12,... | collective-permute-start | bytes 196616 | tf_op jit(solution)/shard_map/ppermute | solution.py:42
  93.7 4.7 %collective-permute-start.13 = (bf16[64,512]{1,0:T(8,128)(2,1)S(1)}, bf16[64,512]{1,0:T(8,128)(2,1)S(1)}, u32[]{:S(2)}, u32[]{:S(2)}) collective-permute-start(bf16[64,512]{1,0:T(8,128)(2,1)S(1)} %add_convert_fusion), channel_id=1, source_target_pairs={{0,4},{2,6},{4,0},{6,2},{1,5},{3,7},{5,1},{7,3},{8,12},{10,14},{12... | collective-permute-start | bytes 196616 | tf_op jit(solution)/shard_map/ppermute | solution.py:42
  95.2 4.9 %collective-permute-start.14 = (bf16[64,512]{1,0:T(8,128)(2,1)S(1)}, bf16[64,512]{1,0:T(8,128)(2,1)S(1)}, u32[]{:S(2)}, u32[]{:S(2)}) collective-permute-start(bf16[64,512]{1,0:T(8,128)(2,1)S(1)} %add_convert_fusion), channel_id=1, source_target_pairs={{0,6},{2,4},{4,2},{6,0},{1,7},{3,5},{5,3},{7,1},{8,14},{10,12},{12... | collective-permute-start | bytes 196616 | tf_op jit(solution)/shard_map/ppermute | solution.py:42
  100.1 3.1 %collective-permute-start.15 = (f32[64,512]{1,0:T(8,128)S(1)}, f32[64,512]{1,0:T(8,128)S(1)}, u32[]{:S(2)}, u32[]{:S(2)}) collective-permute-start(f32[64,512]{1,0:T(8,128)S(1)} %convert_add_fusion.mine_ref), channel_id=1, source_target_pairs={{0,1},{1,0},{2,3},{3,2},{4,5},{5,4},{6,7},{7,6},{8,9},{9,8},{10,11... | collective-permute-start | bytes 393224 | tf_op jit(solution)/shard_map/ppermute | solution.py:42

commit v4 on v3

--- a/solution.py
+++ b/solution.py
@@ -184,18 +184,25 @@
     return jnp.concatenate(pieces, axis=1)
 
 
-def inner_kernel(s_ref, own_ref, other_ref, near_ref, near_half_ref, far_ref, far_half_ref, out_ref):
+SAME = (((1,), (1,)), ((), ()))
+
+
+def inner_own_kernel(s_ref, own_ref, near_ref, near_half_ref, far_ref, far_half_ref, out_ref):
     c = s_ref[0]
-    groups = own_ref.shape[0]
-    rows = groups * ROWS
-    own, other = wide(own_ref, rows), wide(other_ref, rows)
-    dims = (((1,), (1,)), ((), ()))
+    own = wide(own_ref, own_ref.shape[0] * ROWS)
     blocks = [(near_ref, near_half_ref[...])]
     blocks += [(far_ref.at[d], far_half_ref[d : d + 1, :]) for d in range(far_ref.shape[0])]
     for d, (slices, half) in enumerate(blocks):
-        acc = lax.dot_general(own, slices[c], dims, preferred_element_type=jnp.float32)
-        acc += lax.dot_general(other, slices[1 - c], dims, preferred_element_type=jnp.float32)
-        acc = acc - half
+        out_ref[d] = lax.dot_general(own, slices[c], SAME, preferred_element_type=jnp.float32) - half
+
+
+def inner_kernel(s_ref, other_ref, near_ref, far_ref, half_way_ref, out_ref):
+    c = s_ref[0]
+    groups = other_ref.shape[0]
+    other = wide(other_ref, groups * ROWS)
+    for d in range(half_way_ref.shape[0]):
+        slices = far_ref.at[d - 1] if d else near_ref
+        acc = lax.dot_general(other, slices[1 - c], SAME, preferred_element_type=jnp.float32) + half_way_ref[d]
         out_ref[:, d * ROWS : (d + 1) * ROWS, :] = acc.reshape(groups, ROWS, LANES)
 
 
@@ -324,17 +331,27 @@
         flops=4 * (across_x - 1) * orients * degrees * padded,
     )
 
-    partial = call(
-        inner_kernel,
-        shape((groups, across_x * ROWS, LANES)),
+    work = 2 * groups * ROWS * padded * across_x * LANES
+    half_way = call(
+        inner_own_kernel,
+        shape((across_x, groups * ROWS, LANES)),
         scalars,
         mine,
-        other,
         near,
         near_half,
         far,
         far_half,
-        flops=4 * groups * ROWS * padded * across_x * LANES,
+        flops=work,
+    )
+    partial = call(
+        inner_kernel,
+        shape((groups, across_x * ROWS, LANES)),
+        scalars,
+        other,
+        near,
+        far,
+        half_way,
+        flops=work,
     )
     partial = lax.all_to_all(partial, "img", 0, 0, tiled=True)
 

time: 105 us -> 106 us (level)
    pallas_call x9 -> x10, Pallas kernels: 11.9 us -> 12.6 us  [call(): pl.pallas_call(kernel, out_shape=out_shape, in_specs=specs, out_specs=out...]
  transfers between devices with their start and end apart: 18 -> 18, of which waited for: 9 -> 9; matrix products, arithmetic and copies ran while one was open for 0% -> 0% of each run, Pallas kernels for 7% -> 8%
where the time goes in v4:
time: 106 us; the launch traced here: 105 us
  starting transfers between devices  47.8 us (45%)
  waiting for transfers between devices  23.6 us (22%)
  blocking collectives  17 us (16%)
  Pallas kernels  15.8 us (15%)
    ppermute x16, starting transfers between devices, across(): lax.ppermute(x, axis, [(s, s ^ turn) for s in range(lax.axis_size(axis))])  28.7 us
    all_to_all x1, blocking collectives, shards(): partial = lax.all_to_all(partial, 'img', 0, 0, tiled=True)  17 us
    pallas_call x10, Pallas kernels, call(): pl.pallas_call(kernel, out_shape=out_shape, in_specs=specs, out_specs=out...  12.6 us
    all_to_all x1, starting transfers between devices, shards(): lax.all_to_all(cut.reshape(groups, tiles * ROWS, LANES), 'img', 0, 0, til...  12 us
    all_to_all x1, waiting for transfers between devices, shards(): lax.all_to_all(cut.reshape(groups, tiles * ROWS, LANES), 'img', 0, 0, til...  9.66 us
    ppermute x16, waiting for transfers between devices, across(): lax.ppermute(x, axis, [(s, s ^ turn) for s in range(lax.axis_size(axis))])  7.97 us
    all_to_all x1, starting transfers between devices, shards(): posts = lax.all_to_all(copies, ('img', 'x'), 0, 0, tiled=True)  7.07 us
    all_to_all x1, waiting for transfers between devices, shards(): posts = lax.all_to_all(copies, ('img', 'x'), 0, 0, tiled=True)  6.01 us
  transfers between devices with their start and end apart: 18, of which 9 were waited for; matrix products, arithmetic and copies ran while one was open for 0% of the time, Pallas kernels for 8%

profile of v4, /device:TPU:1, one launch (start us, length us, event | category | flops | bytes accessed | tf_op | source)
XLA Modules:
  0.0 105.2 jit_solution(4565673832358961537)
XLA Ops:
  0.7 3.2 %shard_map.94 = bf16[32,4,8,128]{3,2,1,0:T(8,128)(2,1)} custom-call(s32[32]{0:T(128)} %shifts_ref.1, bf16[32,2,16256]{2,1,0:T(2,128)(2,1)} %images_ref.1), custom_call_target="tpu_custom_call" | custom-call | tf_op jit(solution)/shard_map/pallas_call | solution.py:106
  3.9 12.0 %all-to-all-start = ((bf16[32,32,128]{2,1,0:T(8,128)(2,1)}), bf16[32,32,128]{2,1,0:T(8,128)(2,1)S(1)}, u32[]{:S(2)}, u32[]{:S(2)}) async-start(bf16[32,32,128]{2,1,0:T(8,128)(2,1)} %bitcast.24), calls=%async_computation | async-start | bytes 524288 | tf_op jit(solution)/shard_map/all_to_all | solution.py:300
  15.9 9.7 %all-to-all-done.own_ref.refs_0_ = bf16[32,32,128]{2,1,0:T(8,128)(2,1)S(1)} async-done(((bf16[32,32,128]{2,1,0:T(8,128)(2,1)}), bf16[32,32,128]{2,1,0:T(8,128)(2,1)S(1)}, u32[]{:S(2)}, u32[]{:S(2)}) %all-to-all-start) | async-done | bytes 262176 | tf_op jit(solution)/shard_map/all_to_all | solution.py:300
  25.6 3.7 %collective-permute-start = (bf16[32,32,128]{2,1,0:T(8,128)(2,1)S(1)}, bf16[32,32,128]{2,1,0:T(8,128)(2,1)S(1)}, u32[]{:S(2)}, u32[]{:S(2)}) collective-permute-start(bf16[32,32,128]{2,1,0:T(8,128)(2,1)S(1)} %all-to-all-done.own_ref.refs_0_), channel_id=1, source_target_pairs={{0,1},{1,0},{2,3},{3,2},{4,5},{5,4},{6,7},{7,6},{8,9},{9,8},{10,11... | collective-permute-start | bytes 786440 | tf_op jit(solution)/shard_map/ppermute | solution.py:42
  30.6 2.5 %collective-permute-start.2 = (bf16[80,128]{1,0:T(8,128)(2,1)S(1)}, bf16[80,128]{1,0:T(8,128)(2,1)S(1)}, u32[]{:S(2)}, u32[]{:S(2)}) collective-permute-start(bf16[80,128]{1,0:T(8,128)(2,1)S(1)} %pad_maximum_fusion.1.packed_ref), channel_id=1, source_target_pairs={{0,4},{2,6},{4,0},{6,2},{1,5},{3,7},{5,1},{7,3},{8,12},{10,14},{12... | collective-permute-start | bytes 61448 | tf_op jit(solution)/shard_map/ppermute | solution.py:42
  34.9 2.0 %collective-permute-done.3.refs_2_ = bf16[80,128]{1,0:T(8,128)(2,1)S(1)} collective-permute-done((bf16[80,128]{1,0:T(8,128)(2,1)S(1)}, bf16[80,128]{1,0:T(8,128)(2,1)S(1)}, u32[]{:S(2)}, u32[]{:S(2)}) %collective-permute-start.3) | collective-permute-done | bytes 20512 | tf_op jit(solution)/shard_map/ppermute | solution.py:42
  36.9 2.0 %shard_map.96 = (bf16[3,2,128,512]{3,2,1,0:T(8,128)(2,1)S(1)}, f32[3,128]{1,0:T(4,128)S(1)}) custom-call(s32[3]{0:T(128)S(1)} %pad_add_fusion.s_ref._, bf16[2,64,512]{2,1,0:T(8,128)(2,1)S(1)} %pad.9.volume_ref, bf16[80,128]{1,0:T(8,128)(2,1)S(1)} %collective-permute-done.1.refs_0_, bf16[80,128]{1,0:T(8,128)(2,1)S(1)} %collective-permute-done.2.refs_1_, ...), custom_call_target="tpu_custom_call" | custom-call | flops 50331648 | bytes 980480 | tf_op jit(solution)/shard_map/pallas_call | solution.py:27
  40.9 17.0 %all_to_all.15.parts_ref = f32[32,32,128]{2,1,0:T(8,128)S(1)} all-to-all(f32[32,32,128]{2,1,0:T(8,128)S(1)} %shard_map.98), channel_id=1, replica_groups=mesh['img'=32,'x'=4,'c'=2] {'img'}, dimensions={0} | all-to-all | bytes 1048576 | tf_op jit(solution)/shard_map/all_to_all | solution.py:356
  58.7 5.1 %collective-permute-start.4 = (f32[2,8,128]{2,1,0:T(8,128)S(1)}, f32[2,8,128]{2,1,0:T(8,128)S(1)}, u32[]{:S(2)}, u32[]{:S(2)}) collective-permute-start(f32[2,8,128]{2,1,0:T(8,128)S(1)} %get-tuple-element.23.mine_ref), channel_id=1, source_target_pairs={{0,1},{1,0},{2,3},{3,2},{4,5},{5,4},{6,7},{7,6},{8,9},{9,8},{10,11... | collective-permute-start | bytes 24584 | tf_op jit(solution)/shard_map/ppermute | solution.py:42
  64.3 3.3 %collective-permute-start.6 = (bf16[32,32,128]{2,1,0:T(8,128)(2,1)S(1)}, bf16[32,32,128]{2,1,0:T(8,128)(2,1)S(1)}, u32[]{:S(2)}, u32[]{:S(2)}) collective-permute-start(bf16[32,32,128]{2,1,0:T(8,128)(2,1)S(1)} %all-to-all-done.own_ref.refs_0_), channel_id=1, source_target_pairs={{0,4},{2,6},{4,0},{6,2},{1,5},{3,7},{5,1},{7,3},{8,12},{10,14},{12... | collective-permute-start | bytes 786440 | tf_op jit(solution)/shard_map/ppermute | solution.py:42
  67.6 1.3 %shard_map.100 = bf16[32,4,8,128]{3,2,1,0:T(8,128)(2,1)} custom-call(s32[3]{0:T(128)S(1)} %pad_add_fusion.s_ref._, f32[32,128]{1,0:T(8,128)S(1)} %get-tuple-element.22.held_ref, f32[32,128]{1,0:T(8,128)S(1)} %get-tuple-element.21.allowed_ref, f32[2,8,128]{2,1,0:T(8,128)S(1)} %get-tuple-element.23.mine_ref, f32[2,8,128]{2,1,0:T(8,128)S(1)} %collective-permute-done.4.theirs_ref), custom_call_target="tpu_custom_call" | custom-call | bytes 311296 | tf_op jit(solution)/shard_map/pallas_call | solution.py:27
  68.9 7.1 %all-to-all-start.2 = ((bf16[128,8,128]{2,1,0:T(8,128)(2,1)}), bf16[128,8,128]{2,1,0:T(8,128)(2,1)S(1)}, u32[]{:S(2)}, u32[]{:S(2)}) async-start(bf16[128,8,128]{2,1,0:T(8,128)(2,1)} %bitcast.10), calls=%async_computation.2 | async-start | bytes 524288 | tf_op jit(solution)/shard_map/all_to_all | solution.py:371
  76.0 1.3 %collective-permute-start.10 = (bf16[32,32,128]{2,1,0:T(8,128)(2,1)S(1)}, bf16[32,32,128]{2,1,0:T(8,128)(2,1)S(1)}, u32[]{:S(2)}, u32[]{:S(2)}) collective-permute-start(bf16[32,32,128]{2,1,0:T(8,128)(2,1)S(1)} %collective-permute-done.7.refs_3_), channel_id=1, source_target_pairs={{0,1},{1,0},{2,3},{3,2},{4,5},{5,4},{6,7},{7,6},{8,9},{9,8},{10,11... | collective-permute-start | bytes 786440 | tf_op jit(solution)/shard_map/ppermute | solution.py:42
  77.4 1.8 %collective-permute-done.6.refs_2_ = bf16[32,32,128]{2,1,0:T(8,128)(2,1)S(1)} collective-permute-done((bf16[32,32,128]{2,1,0:T(8,128)(2,1)S(1)}, bf16[32,32,128]{2,1,0:T(8,128)(2,1)S(1)}, u32[]{:S(2)}, u32[]{:S(2)}) %collective-permute-start.6) | collective-permute-done | bytes 262176 | tf_op jit(solution)/shard_map/ppermute | solution.py:42
  79.3 1.6 %collective-permute-start.9 = (bf16[32,32,128]{2,1,0:T(8,128)(2,1)S(1)}, bf16[32,32,128]{2,1,0:T(8,128)(2,1)S(1)}, u32[]{:S(2)}, u32[]{:S(2)}) collective-permute-start(bf16[32,32,128]{2,1,0:T(8,128)(2,1)S(1)} %collective-permute-done.6.refs_2_), channel_id=1, source_target_pairs={{0,1},{1,0},{2,3},{3,2},{4,5},{5,4},{6,7},{7,6},{8,9},{9,8},{10,11... | collective-permute-start | bytes 786440 | tf_op jit(solution)/shard_map/ppermute | solution.py:42
  82.0 6.0 %all-to-all-done.2 = bf16[128,8,128]{2,1,0:T(8,128)(2,1)S(1)} async-done(((bf16[128,8,128]{2,1,0:T(8,128)(2,1)}), bf16[128,8,128]{2,1,0:T(8,128)(2,1)S(1)}, u32[]{:S(2)}, u32[]{:S(2)}) %all-to-all-start.2) | async-done | bytes 262176 | tf_op jit(solution)/shard_map/all_to_all | solution.py:371
  88.0 1.6 %shard_map.102 = (f32[2,128,512]{2,1,0:T(8,128)S(1)}, f32[64,512]{1,0:T(8,128)S(1)}, bf16[64,512]{1,0:T(8,128)(2,1)S(1)}) custom-call(s32[3]{0:T(128)S(1)} %pad_add_fusion.s_ref._, bf16[32,4,8,128]{3,2,1,0:T(8,128)(2,1)S(1)} %bitcast.20, bf16[2,128,512]{2,1,0:T(8,128)(2,1)S(1)} %get-tuple-element.16.near_ref.slices_ref, ...), custom_call_target="tpu_custom_call" | custom-call | flops 268435456 | bytes 3506176 | tf_op jit(solution)/shard_map/pallas_call | solution.py:27
  89.6 3.6 %collective-permute-start.11 = (bf16[64,512]{1,0:T(8,128)(2,1)S(1)}, bf16[64,512]{1,0:T(8,128)(2,1)S(1)}, u32[]{:S(2)}, u32[]{:S(2)}) collective-permute-start(bf16[64,512]{1,0:T(8,128)(2,1)S(1)} %get-tuple-element.28), channel_id=1, source_target_pairs={{0,1},{1,0},{2,3},{3,2},{4,5},{5,4},{6,7},{7,6},{8,9},{9,8},{10,11... | collective-permute-start | bytes 196616 | tf_op jit(solution)/shard_map/ppermute | solution.py:42
  94.4 1.5 %collective-permute-start.13 = (bf16[64,512]{1,0:T(8,128)(2,1)S(1)}, bf16[64,512]{1,0:T(8,128)(2,1)S(1)}, u32[]{:S(2)}, u32[]{:S(2)}) collective-permute-start(bf16[64,512]{1,0:T(8,128)(2,1)S(1)} %add_convert_fusion), channel_id=1, source_target_pairs={{0,4},{2,6},{4,0},{6,2},{1,5},{3,7},{5,1},{7,3},{8,12},{10,14},{12... | collective-permute-start | bytes 196616 | tf_op jit(solution)/shard_map/ppermute | solution.py:42
  95.9 2.2 %collective-permute-start.14 = (bf16[64,512]{1,0:T(8,128)(2,1)S(1)}, bf16[64,512]{1,0:T(8,128)(2,1)S(1)}, u32[]{:S(2)}, u32[]{:S(2)}) collective-permute-start(bf16[64,512]{1,0:T(8,128)(2,1)S(1)} %add_convert_fusion), channel_id=1, source_target_pairs={{0,6},{2,4},{4,2},{6,0},{1,7},{3,5},{5,3},{7,1},{8,14},{10,12},{12... | collective-permute-start | bytes 196616 | tf_op jit(solution)/shard_map/ppermute | solution.py:42
  99.0 1.8 %collective-permute-done.14 = bf16[64,512]{1,0:T(8,128)(2,1)S(1)} collective-permute-done((bf16[64,512]{1,0:T(8,128)(2,1)S(1)}, bf16[64,512]{1,0:T(8,128)(2,1)S(1)}, u32[]{:S(2)}, u32[]{:S(2)}) %collective-permute-start.14) | collective-permute-done | bytes 65568 | tf_op jit(solution)/shard_map/ppermute | solution.py:42
  100.8 1.6 %collective-permute-start.15 = (f32[64,512]{1,0:T(8,128)S(1)}, f32[64,512]{1,0:T(8,128)S(1)}, u32[]{:S(2)}, u32[]{:S(2)}) collective-permute-start(f32[64,512]{1,0:T(8,128)S(1)} %convert_add_fusion.mine_ref), channel_id=1, source_target_pairs={{0,1},{1,0},{2,3},{3,2},{4,5},{5,4},{6,7},{7,6},{8,9},{9,8},{10,11... | collective-permute-start | bytes 393224 | tf_op jit(solution)/shard_map/ppermute | solution.py:42
  102.4 1.5 %shard_map.103 = (f32[1016,128]{1,0:T(8,128)}, f32[32,128]{1,0:T(8,128)}) custom-call(s32[3]{0:T(128)S(1)} %pad_add_fusion.s_ref._, f32[2,128,512]{2,1,0:T(8,128)S(1)} %get-tuple-element.24.sums_ref, bf16[32,32,128]{2,1,0:T(8,128)(2,1)S(1)} %bitcast.21), custom_call_target="tpu_custom_call" | custom-call | bytes 1323008 | tf_op jit(solution)/shard_map/pallas_call | solution.py:27
  103.9 1.3 %shard_map.104 = f32[64,2,508]{2,1,0:T(2,128)} custom-call(s32[3]{0:T(128)S(1)} %pad_add_fusion.s_ref._, f32[64,512]{1,0:T(8,128)S(1)} %convert_add_fusion.mine_ref, f32[64,512]{1,0:T(8,128)S(1)} %collective-permute-done.15.theirs_ref), custom_call_target="tpu_custom_call" | custom-call | bytes 522240 | tf_op jit(solution)/shard_map/pallas_call | solution.py:27
  (43 shorter events, 9.8 us)
Async XLA Ops:
  0.6 15.3 %copy-start.1 = (f32[128]{0:T(128)S(1)}, f32[128]{0:T(128)}, u32[]{:S(2)}) copy-start(f32[128]{0:T(128)} %param.13) | copy-start | bytes 1540
  0.6 28.7 %copy-start.4 = (bf16[128,64]{0,1:T(8,128)(2,1)S(1)}, bf16[128,64]{0,1:T(8,128)(2,1)}, u32[]{:S(2)}) copy-start(bf16[128,64]{0,1:T(8,128)(2,1)} %param.12) | copy-start | bytes 49156
  0.7 32.7 %copy-start.3 = (bf16[64,2,508]{2,1,0:T(2,128)(2,1)S(1)}, bf16[64,2,508]{2,1,0:T(2,128)(2,1)}, u32[]{:S(2)}) copy-start(bf16[64,2,508]{2,1,0:T(2,128)(2,1)} %param.11) | copy-start | bytes 390148
  0.7 32.7 %copy-start = (s32[1,512]{1,0:T(1,128)S(1)}, s32[1,512]{1,0:T(1,128)}, u32[]{:S(2)}) copy-start(s32[1,512]{1,0:T(1,128)} %param.10) | copy-start | bytes 6148
  0.7 32.7 %copy-start.2 = (f32[32]{0:T(128)S(1)}, f32[32]{0:T(128)}, u32[]{:S(2)}) copy-start(f32[32]{0:T(128)} %temp_ref.1) | copy-start | bytes 388
  3.9 21.7 %all-to-all-start = ((bf16[32,32,128]{2,1,0:T(8,128)(2,1)}), bf16[32,32,128]{2,1,0:T(8,128)(2,1)S(1)}, u32[]{:S(2)}, u32[]{:S(2)}) async-start(bf16[32,32,128]{2,1,0:T(8,128)(2,1)} %bitcast.24), calls=%async_computation | async-start | bytes 524288 | tf_op jit(solution)/shard_map/all_to_all | solution.py:300
  25.6 14.4 %collective-permute-start = (bf16[32,32,128]{2,1,0:T(8,128)(2,1)S(1)}, bf16[32,32,128]{2,1,0:T(8,128)(2,1)S(1)}, u32[]{:S(2)}, u32[]{:S(2)}) collective-permute-start(bf16[32,32,128]{2,1,0:T(8,128)(2,1)S(1)} %all-to-all-done.own_ref.refs_0_), channel_id=1, source_target_pairs={{0,1},{1,0},{2,3},{3,2},{4,5},{5,4},{6,7},{7,6},{8,9},{9,8},{10,11... | collective-permute-start | bytes 786440 | tf_op jit(solution)/shard_map/ppermute | solution.py:42
  29.3 5.3 %collective-permute-start.1 = (bf16[80,128]{1,0:T(8,128)(2,1)S(1)}, bf16[80,128]{1,0:T(8,128)(2,1)S(1)}, u32[]{:S(2)}, u32[]{:S(2)}) collective-permute-start(bf16[80,128]{1,0:T(8,128)(2,1)S(1)} %pad_maximum_fusion.1.packed_ref), channel_id=1, source_target_pairs={{0,2},{2,0},{4,6},{6,4},{1,3},{3,1},{5,7},{7,5},{8,10},{10,8},{12,... | collective-permute-start | bytes 61448 | tf_op jit(solution)/shard_map/ppermute | solution.py:42
  30.6 4.3 %collective-permute-start.2 = (bf16[80,128]{1,0:T(8,128)(2,1)S(1)}, bf16[80,128]{1,0:T(8,128)(2,1)S(1)}, u32[]{:S(2)}, u32[]{:S(2)}) collective-permute-start(bf16[80,128]{1,0:T(8,128)(2,1)S(1)} %pad_maximum_fusion.1.packed_ref), channel_id=1, source_target_pairs={{0,4},{2,6},{4,0},{6,2},{1,5},{3,7},{5,1},{7,3},{8,12},{10,14},{12... | collective-permute-start | bytes 61448 | tf_op jit(solution)/shard_map/ppermute | solution.py:42
  33.1 3.8 %collective-permute-start.3 = (bf16[80,128]{1,0:T(8,128)(2,1)S(1)}, bf16[80,128]{1,0:T(8,128)(2,1)S(1)}, u32[]{:S(2)}, u32[]{:S(2)}) collective-permute-start(bf16[80,128]{1,0:T(8,128)(2,1)S(1)} %pad_maximum_fusion.1.packed_ref), channel_id=1, source_target_pairs={{0,6},{2,4},{4,2},{6,0},{1,7},{3,5},{5,3},{7,1},{8,14},{10,12},{12... | collective-permute-start | bytes 61448 | tf_op jit(solution)/shard_map/ppermute | solution.py:42
  58.7 8.9 %collective-permute-start.4 = (f32[2,8,128]{2,1,0:T(8,128)S(1)}, f32[2,8,128]{2,1,0:T(8,128)S(1)}, u32[]{:S(2)}, u32[]{:S(2)}) collective-permute-start(f32[2,8,128]{2,1,0:T(8,128)S(1)} %get-tuple-element.23.mine_ref), channel_id=1, source_target_pairs={{0,1},{1,0},{2,3},{3,2},{4,5},{5,4},{6,7},{7,6},{8,9},{9,8},{10,11... | collective-permute-start | bytes 24584 | tf_op jit(solution)/shard_map/ppermute | solution.py:42
  63.8 12.2 %collective-permute-start.7 = (bf16[32,32,128]{2,1,0:T(8,128)(2,1)S(1)}, bf16[32,32,128]{2,1,0:T(8,128)(2,1)S(1)}, u32[]{:S(2)}, u32[]{:S(2)}) collective-permute-start(bf16[32,32,128]{2,1,0:T(8,128)(2,1)S(1)} %all-to-all-done.own_ref.refs_0_), channel_id=1, source_target_pairs={{0,6},{2,4},{4,2},{6,0},{1,7},{3,5},{5,3},{7,1},{8,14},{10,12},{12... | collective-permute-start | bytes 786440 | tf_op jit(solution)/shard_map/ppermute | solution.py:42
  64.3 13.0 %collective-permute-start.5 = (bf16[32,32,128]{2,1,0:T(8,128)(2,1)S(1)}, bf16[32,32,128]{2,1,0:T(8,128)(2,1)S(1)}, u32[]{:S(2)}, u32[]{:S(2)}) collective-permute-start(bf16[32,32,128]{2,1,0:T(8,128)(2,1)S(1)} %all-to-all-done.own_ref.refs_0_), channel_id=1, source_target_pairs={{0,2},{2,0},{4,6},{6,4},{1,3},{3,1},{5,7},{7,5},{8,10},{10,8},{12,... | collective-permute-start | bytes 786440 | tf_op jit(solution)/shard_map/ppermute | solution.py:42
  64.3 15.0 %collective-permute-start.6 = (bf16[32,32,128]{2,1,0:T(8,128)(2,1)S(1)}, bf16[32,32,128]{2,1,0:T(8,128)(2,1)S(1)}, u32[]{:S(2)}, u32[]{:S(2)}) collective-permute-start(bf16[32,32,128]{2,1,0:T(8,128)(2,1)S(1)} %all-to-all-done.own_ref.refs_0_), channel_id=1, source_target_pairs={{0,4},{2,6},{4,0},{6,2},{1,5},{3,7},{5,1},{7,3},{8,12},{10,14},{12... | collective-permute-start | bytes 786440 | tf_op jit(solution)/shard_map/ppermute | solution.py:42
  68.9 19.1 %all-to-all-start.2 = ((bf16[128,8,128]{2,1,0:T(8,128)(2,1)}), bf16[128,8,128]{2,1,0:T(8,128)(2,1)S(1)}, u32[]{:S(2)}, u32[]{:S(2)}) async-start(bf16[128,8,128]{2,1,0:T(8,128)(2,1)} %bitcast.10), calls=%async_computation.2 | async-start | bytes 524288 | tf_op jit(solution)/shard_map/all_to_all | solution.py:371
  76.0 5.7 %collective-permute-start.10 = (bf16[32,32,128]{2,1,0:T(8,128)(2,1)S(1)}, bf16[32,32,128]{2,1,0:T(8,128)(2,1)S(1)}, u32[]{:S(2)}, u32[]{:S(2)}) collective-permute-start(bf16[32,32,128]{2,1,0:T(8,128)(2,1)S(1)} %collective-permute-done.7.refs_3_), channel_id=1, source_target_pairs={{0,1},{1,0},{2,3},{3,2},{4,5},{5,4},{6,7},{7,6},{8,9},{9,8},{10,11... | collective-permute-start | bytes 786440 | tf_op jit(solution)/shard_map/ppermute | solution.py:42
  77.3 4.4 %collective-permute-start.8 = (bf16[32,32,128]{2,1,0:T(8,128)(2,1)S(1)}, bf16[32,32,128]{2,1,0:T(8,128)(2,1)S(1)}, u32[]{:S(2)}, u32[]{:S(2)}) collective-permute-start(bf16[32,32,128]{2,1,0:T(8,128)(2,1)S(1)} %collective-permute-done.5.refs_1_), channel_id=1, source_target_pairs={{0,1},{1,0},{2,3},{3,2},{4,5},{5,4},{6,7},{7,6},{8,9},{9,8},{10,11... | collective-permute-start | bytes 786440 | tf_op jit(solution)/shard_map/ppermute | solution.py:42
  79.3 2.7 %collective-permute-start.9 = (bf16[32,32,128]{2,1,0:T(8,128)(2,1)S(1)}, bf16[32,32,128]{2,1,0:T(8,128)(2,1)S(1)}, u32[]{:S(2)}, u32[]{:S(2)}) collective-permute-start(bf16[32,32,128]{2,1,0:T(8,128)(2,1)S(1)} %collective-permute-done.6.refs_2_), channel_id=1, source_target_pairs={{0,1},{1,0},{2,3},{3,2},{4,5},{5,4},{6,7},{7,6},{8,9},{9,8},{10,11... | collective-permute-start | bytes 786440 | tf_op jit(solution)/shard_map/ppermute | solution.py:42
  89.6 4.5 %collective-permute-start.11 = (bf16[64,512]{1,0:T(8,128)(2,1)S(1)}, bf16[64,512]{1,0:T(8,128)(2,1)S(1)}, u32[]{:S(2)}, u32[]{:S(2)}) collective-permute-start(bf16[64,512]{1,0:T(8,128)(2,1)S(1)} %get-tuple-element.28), channel_id=1, source_target_pairs={{0,1},{1,0},{2,3},{3,2},{4,5},{5,4},{6,7},{7,6},{8,9},{9,8},{10,11... | collective-permute-start | bytes 196616 | tf_op jit(solution)/shard_map/ppermute | solution.py:42
  94.1 3.9 %collective-permute-start.12 = (bf16[64,512]{1,0:T(8,128)(2,1)S(1)}, bf16[64,512]{1,0:T(8,128)(2,1)S(1)}, u32[]{:S(2)}, u32[]{:S(2)}) collective-permute-start(bf16[64,512]{1,0:T(8,128)(2,1)S(1)} %add_convert_fusion), channel_id=1, source_target_pairs={{0,2},{2,0},{4,6},{6,4},{1,3},{3,1},{5,7},{7,5},{8,10},{10,8},{12,... | collective-permute-start | bytes 196616 | tf_op jit(solution)/shard_map/ppermute | solution.py:42
  94.4 4.7 %collective-permute-start.13 = (bf16[64,512]{1,0:T(8,128)(2,1)S(1)}, bf16[64,512]{1,0:T(8,128)(2,1)S(1)}, u32[]{:S(2)}, u32[]{:S(2)}) collective-permute-start(bf16[64,512]{1,0:T(8,128)(2,1)S(1)} %add_convert_fusion), channel_id=1, source_target_pairs={{0,4},{2,6},{4,0},{6,2},{1,5},{3,7},{5,1},{7,3},{8,12},{10,14},{12... | collective-permute-start | bytes 196616 | tf_op jit(solution)/shard_map/ppermute | solution.py:42
  95.9 4.9 %collective-permute-start.14 = (bf16[64,512]{1,0:T(8,128)(2,1)S(1)}, bf16[64,512]{1,0:T(8,128)(2,1)S(1)}, u32[]{:S(2)}, u32[]{:S(2)}) collective-permute-start(bf16[64,512]{1,0:T(8,128)(2,1)S(1)} %add_convert_fusion), channel_id=1, source_target_pairs={{0,6},{2,4},{4,2},{6,0},{1,7},{3,5},{5,3},{7,1},{8,14},{10,12},{12... | collective-permute-start | bytes 196616 | tf_op jit(solution)/shard_map/ppermute | solution.py:42
  100.8 3.1 %collective-permute-start.15 = (f32[64,512]{1,0:T(8,128)S(1)}, f32[64,512]{1,0:T(8,128)S(1)}, u32[]{:S(2)}, u32[]{:S(2)}) collective-permute-start(f32[64,512]{1,0:T(8,128)S(1)} %convert_add_fusion.mine_ref), channel_id=1, source_target_pairs={{0,1},{1,0},{2,3},{3,2},{4,5},{5,4},{6,7},{7,6},{8,9},{9,8},{10,11... | collective-permute-start | bytes 393224 | tf_op jit(solution)/shard_map/ppermute | solution.py:42
